TPU v7x, 512 devices: a whole 4x4x16 slice. The times are simulated.
512 devices in a mesh: shot: 4 (over x), gx: 16 (over z_hi, y), gy: 8 (over z_lo, core).
Axes of the slice: x: 4, y: 4, z: 16 (z_hi: 4, z_lo: 4; z = z_hi * 4 + z_lo), core: 2. Of those that a mesh axis runs over, the one named last changes fastest.
Arguments:
- forward_now: float32 [4, 512, 256, 128], P('shot', 'gx', 'gy'), may hold values from -3 to 3
- forward_later: float32 [4, 512, 256, 128], P('shot', 'gx', 'gy'), may hold values from -3 to 3
- adjoint_now: float32 [4, 512, 256, 128], P('shot', 'gx', 'gy'), may hold values from -3 to 3
- adjoint_later: float32 [4, 512, 256, 128], P('shot', 'gx', 'gy'), may hold values from -3 to 3
- courant: float32 [512, 256, 128], P('gx', 'gy'), may hold values from 0.15 to 0.45
- source_cells: int32 [4, 16, 3], P('shot'), may hold values from 0 to 511, as said below
- source_wave: float32 [4, 3, 16], P('shot'), may hold values from -6 to 6
- receiver_cells: int32 [4, 4096, 3], P('shot'), may hold values from 0 to 511, as said below
- residual: float32 [4, 3, 4096], P('shot'), may hold values from -6 to 6
Outputs:
- forward_first: float32 [4, 512, 256, 128], P('shot', 'gx', 'gy')
- adjoint_first: float32 [4, 512, 256, 128], P('shot', 'gx', 'gy')
- gradient: float32 [512, 256, 128], P('gx', 'gy')
Inputs may be any that keep to these rules, and one draw needn't show every extreme that they name: `source_cells`: entry [s, i] holds the first, second and depth cell index of source i of shot group s, each inside the grid of 512 x 256 x 128 cells; cells may repeat. `receiver_cells`: entry [s, r] holds the first, second and depth cell index of receiver r of shot group s, each inside the grid of 512 x 256 x 128 cells; cells may repeat.
All inputs are finite; a program needn't handle non-finite values.
Results may differ from a plain program's by a relative error of at most 0.0003.
Values sent between devices are 32-bit elements; how exact they have to be, the bound alone decides.
A program may use at most 64 MiB of HBM per device.

v0:
```python
import math

import jax
import jax.numpy as jnp
from jax import lax
from jax.sharding import PartitionSpec as P

STEPS = 3


COEFFS = (-205.0 / 72.0, 8.0 / 5.0, -1.0 / 5.0, 8.0 / 315.0, -1.0 / 560.0)
GRAD_SCALE = 0.1


def extended_2(block, sides, width):
    for axis, dim in sides:
        count = lax.axis_size(axis)
        forward = [(i, i + 1) for i in range(count - 1)]
        backward = [(target, source) for source, target in forward]
        low = lax.ppermute(
            lax.slice_in_dim(block, block.shape[dim] - width, None, axis=dim), axis, forward
        )
        high = lax.ppermute(lax.slice_in_dim(block, 0, width, axis=dim), axis, backward)
        block = jnp.concatenate([low, block, high], axis=dim)
    return block


def stencil(extended):
    full = jnp.pad(extended, [(0, 0)] * (extended.ndim - 1) + [(4, 4)])
    rows_x = extended.shape[-3] - 8
    rows_y = extended.shape[-2] - 8
    depth = extended.shape[-1]

    def shifted(step_x, step_y, step_z):
        return full[
            ...,
            4 + step_x : 4 + step_x + rows_x,
            4 + step_y : 4 + step_y + rows_y,
            4 + step_z : 4 + step_z + depth,
        ]

    summed = 3.0 * COEFFS[0] * shifted(0, 0, 0)
    for reach in range(1, 5):
        pairs = (
            shifted(reach, 0, 0)
            + shifted(-reach, 0, 0)
            + (shifted(0, reach, 0) + shifted(0, -reach, 0))
        )
        pairs = pairs + (shifted(0, 0, reach) + shifted(0, 0, -reach))
        summed = summed + COEFFS[reach] * pairs
    return summed


def inject(stacked, which, cells, values, start_x, start_y):
    extent_x = stacked.shape[1]
    extent_y = stacked.shape[2]
    depth = stacked.shape[3]
    count = cells.shape[0]
    block = math.gcd(count, 512)
    blocks = count // block
    cell_blocks = cells.reshape(blocks, block, 3)
    value_blocks = values.reshape(blocks, block)
    range_x = jnp.arange(extent_x, dtype=jnp.int32)
    range_y = jnp.arange(extent_y, dtype=jnp.int32)
    range_z = jnp.arange(depth, dtype=jnp.int32)

    def one_block(total, items):
        chosen, amounts = items
        hit_x = jnp.where(chosen[:, 0:1] - start_x == range_x[None, :], amounts[:, None], 0.0)
        hit_y = (chosen[:, 1:2] - start_y == range_y[None, :]).astype(jnp.float32)
        hit_z = (chosen[:, 2:3] == range_z[None, :]).astype(jnp.float32)
        plane = (hit_x[:, :, None] * hit_y[:, None, :]).reshape(block, extent_x * extent_y)
        added = lax.dot_general(
            plane,
            hit_z,
            (((0,), (0,)), ((), ())),
            precision=lax.Precision.HIGHEST,
            preferred_element_type=jnp.float32,
        )
        return (total + added, None)

    start = jnp.zeros((extent_x * extent_y, depth), jnp.float32)
    total, unused = lax.scan(one_block, start, (cell_blocks, value_blocks))
    return stacked.at[which].add(total.reshape(extent_x, extent_y, depth))


def add_term(summed, term):
    return summed + term


def shards(
    forward_now,
    forward_later,
    adjoint_now,
    adjoint_later,
    courant,
    source_cells,
    source_wave,
    receiver_cells,
    residual,
):
    rows_x = courant.shape[0]
    rows_y = courant.shape[1]
    anchor_x = lax.axis_index("gx") * rows_x
    anchor_y = lax.axis_index("gy") * rows_y
    sources = source_cells[0]
    amplitude = source_wave[0]
    receivers = receiver_cells[0]
    misfit = residual[0]
    summed = jnp.zeros(courant.shape, jnp.float32)
    current = jnp.concatenate([forward_now, adjoint_now], 0)
    later = jnp.concatenate([forward_later, adjoint_later], 0)
    squared = courant * courant
    for step in range(STEPS):
        extended = extended_2(current, (("gx", 1), ("gy", 2)), 4)
        curved = stencil(extended)
        term = 2.0 * courant * current[1] * curved[0]
        summed = add_term(summed, term)
        earlier = 2.0 * current - later + squared * curved
        earlier = inject(earlier, 0, sources, amplitude[step], anchor_x, anchor_y)
        earlier = inject(earlier, 1, receivers, misfit[step], anchor_x, anchor_y)
        later = current
        current = earlier
    gradient = lax.psum(summed, "shot")
    return (current[0:1], current[1:2], GRAD_SCALE * gradient)


def solution(mesh):
    placed = (
        P("shot", "gx", "gy", None),
        P("shot", "gx", "gy", None),
        P("shot", "gx", "gy", None),
        P("shot", "gx", "gy", None),
        P("gx", "gy", None),
        P("shot", None, None),
        P("shot", None, None),
        P("shot", None, None),
        P("shot", None, None),
    )
    return jax.shard_map(
        shards,
        mesh=mesh,
        in_specs=placed,
        out_specs=(P("shot", "gx", "gy", None), P("shot", "gx", "gy", None), P("gx", "gy", None)),
        check_vma=False,
    )
```

profile of v0, /device:TPU:8, one launch (start us, length us, event | category | flops | bytes accessed | tf_op | source)
XLA Modules:
  0.0 263.9 jit_solution(13298024963650580862)
XLA Ops:
  10.3 7.7 %collective-permute-start = (f32[2,4,32,128]{3,2,1,0:T(8,128)}, f32[2,4,32,128]{3,2,1,0:T(8,128)S(1)}, u32[]{:S(2)}, u32[]{:S(2)}) collective-permute-start(f32[2,4,32,128]{3,2,1,0:T(8,128)} %get-tuple-element.641), channel_id=1, source_target_pairs={{8,0},{16,8},{24,16},{32,24},{40,32},{48,40},{56,48},{64,56},{72,6... | collective-permute-start | bytes 393224 | tf_op jit(solution)/shard_map/ppermute | solution.py:23
  22.3 25.7 %while.60 = (s32[]{:T(128)}, f32[1024,128]{1,0:T(8,128)}, s32[8,512,3]{1,2,0:T(4,128)S(1)}, s32[]{:T(128)}, f32[8,512]{1,0:T(8,128)S(1)}, /*index=5*/s32[]{:T(128)}, s32[]{:T(128)}, s32[]{:T(128)}) while((s32[]{:T(128)}, f32[1024,128]{1,0:T(8,128)}, s32[8,512,3]{1,2,0:T(4,128)S(1)}, s32[]{:T(128)}, ...), condition=%wide.region_1.2_spmd.clone.clone, body=%wide.region_0.1_spmd.clone.clone.sunk | while | flops 806224896 | bytes 5541999 | solution.py:83
  24.9 3.0 %convolution_add_fusion.6 = f32[1024,128]{1,0:T(8,128)} fusion(f32[512,1024]{0,1:T(8,128)S(1)} %bitcast.147, f32[1024,128]{1,0:T(8,128)} %get-tuple-element.792, pred[]{:T(512)S(6)} %compare.91, s32[512]{0:T(512)S(1)} %bitcast.159), kind=kOutput, calls=%fused_computation.6.clone.1 | convolution fusion | flops 805634048 | bytes 3147777 | tf_op jit(solution)/shard_map/while/body/eval_jaxpr/dot_general | solution.py:73
  28.3 3.0 %convolution_add_fusion.6 = f32[1024,128]{1,0:T(8,128)} fusion(f32[512,1024]{0,1:T(8,128)S(1)} %bitcast.147, f32[1024,128]{1,0:T(8,128)} %get-tuple-element.792, pred[]{:T(512)S(6)} %compare.91, s32[512]{0:T(512)S(1)} %bitcast.159), kind=kOutput, calls=%fused_computation.6.clone.1 | convolution fusion | flops 805634048 | bytes 3147777 | tf_op jit(solution)/shard_map/while/body/eval_jaxpr/dot_general | solution.py:73
  31.6 3.0 %convolution_add_fusion.6 = f32[1024,128]{1,0:T(8,128)} fusion(f32[512,1024]{0,1:T(8,128)S(1)} %bitcast.147, f32[1024,128]{1,0:T(8,128)} %get-tuple-element.792, pred[]{:T(512)S(6)} %compare.91, s32[512]{0:T(512)S(1)} %bitcast.159), kind=kOutput, calls=%fused_computation.6.clone.1 | convolution fusion | flops 805634048 | bytes 3147777 | tf_op jit(solution)/shard_map/while/body/eval_jaxpr/dot_general | solution.py:73
  34.9 3.0 %convolution_add_fusion.6 = f32[1024,128]{1,0:T(8,128)} fusion(f32[512,1024]{0,1:T(8,128)S(1)} %bitcast.147, f32[1024,128]{1,0:T(8,128)} %get-tuple-element.792, pred[]{:T(512)S(6)} %compare.91, s32[512]{0:T(512)S(1)} %bitcast.159), kind=kOutput, calls=%fused_computation.6.clone.1 | convolution fusion | flops 805634048 | bytes 3147777 | tf_op jit(solution)/shard_map/while/body/eval_jaxpr/dot_general | solution.py:73
  38.3 3.0 %convolution_add_fusion.6 = f32[1024,128]{1,0:T(8,128)} fusion(f32[512,1024]{0,1:T(8,128)S(1)} %bitcast.147, f32[1024,128]{1,0:T(8,128)} %get-tuple-element.792, pred[]{:T(512)S(6)} %compare.91, s32[512]{0:T(512)S(1)} %bitcast.159), kind=kOutput, calls=%fused_computation.6.clone.1 | convolution fusion | flops 805634048 | bytes 3147777 | tf_op jit(solution)/shard_map/while/body/eval_jaxpr/dot_general | solution.py:73
  41.6 3.0 %convolution_add_fusion.6 = f32[1024,128]{1,0:T(8,128)} fusion(f32[512,1024]{0,1:T(8,128)S(1)} %bitcast.147, f32[1024,128]{1,0:T(8,128)} %get-tuple-element.792, pred[]{:T(512)S(6)} %compare.91, s32[512]{0:T(512)S(1)} %bitcast.159), kind=kOutput, calls=%fused_computation.6.clone.1 | convolution fusion | flops 805634048 | bytes 3147777 | tf_op jit(solution)/shard_map/while/body/eval_jaxpr/dot_general | solution.py:73
  45.0 3.0 %convolution_add_fusion.6 = f32[1024,128]{1,0:T(8,128)} fusion(f32[512,1024]{0,1:T(8,128)S(1)} %bitcast.147, f32[1024,128]{1,0:T(8,128)} %get-tuple-element.792, pred[]{:T(512)S(6)} %compare.91, s32[512]{0:T(512)S(1)} %bitcast.159), kind=kOutput, calls=%fused_computation.6.clone.1 | convolution fusion | flops 805634048 | bytes 3147777 | tf_op jit(solution)/shard_map/while/body/eval_jaxpr/dot_general | solution.py:73
  49.5 3.0 %collective-permute-start.3 = (f32[2,40,4,128]{3,2,1,0:T(4,128)S(1)}, f32[2,40,4,128]{3,2,1,0:T(4,128)S(1)}, u32[]{:S(2)}, u32[]{:S(2)}) collective-permute-start(f32[2,40,4,128]{3,2,1,0:T(4,128)S(1)} %get-tuple-element.634), channel_id=1, source_target_pairs={{0,1},{1,2},{2,3},{3,4},{4,5},{5,6},{6,7},{8,9},{9,10},{10,11},{11... | collective-permute-start | bytes 491528 | tf_op jit(solution)/shard_map/ppermute | solution.py:20
  57.4 3.1 %select_maximum_fusion.8 = f32[2,40,40,136]{3,2,1,0:T(8,128)S(1)} fusion(f32[2,40,4,128]{3,2,1,0:T(4,128)} %copy-done.14, f32[2,40,4,128]{3,2,1,0:T(4,128)} %copy-done.15, f32[2,4,32,128]{3,2,1,0:T(8,128)S(1)} %collective-permute-done, f32[2,32,32,128]{3,2,1,0:T(8,128)S(1)} %constant_dynamic-update-slice_fusion, f32[2,4,32,128]{3,2,1,0:T(8,128)S(1)} %collective-permute-done.1), kind=kLoop, calls=%fused_computation.52 | loop fusion | flops 5222400 | bytes 3379200 | tf_op jit(solution)/shard_map/concatenate | solution.py:24
  60.5 6.2 %fusion.105 = (f32[2,32,32,128]{3,2,1,0:T(8,128)S(1)}, f32[2,32,32,128]{3,2,1,0:T(8,128)}) fusion(f32[1,32,32,128]{3,2,1,0:T(8,128)} %param.30, f32[1,32,32,128]{3,2,1,0:T(8,128)} %param.28, f32[2,32,32,128]{3,2,1,0:T(8,128)S(1)} %constant_dynamic-update-slice_fusion, f32[32,32,128]{2,1,0:T(8,128)S(1)} %copy-done.6, ...), kind=kLoop, calls=%fused_computation.216 | loop fusion | flops 11010048 | bytes 21757952 | tf_op jit(solution)/shard_map/add | solution.py:119
  68.5 3.9 %collective-permute-start.4 = (f32[2,4,32,128]{3,2,1,0:T(8,128)S(1)}, f32[2,4,32,128]{3,2,1,0:T(8,128)S(1)}, u32[]{:S(2)}, u32[]{:S(2)}) collective-permute-start(f32[2,4,32,128]{3,2,1,0:T(8,128)S(1)} %get-tuple-element.639), channel_id=1, source_target_pairs={{8,0},{16,8},{24,16},{32,24},{40,32},{48,40},{56,48},{64,56},{72,6... | collective-permute-start | bytes 393224 | tf_op jit(solution)/shard_map/ppermute | solution.py:23
  75.8 3.7 %collective-permute-done.5 = f32[2,4,32,128]{3,2,1,0:T(8,128)S(1)} collective-permute-done((f32[2,4,32,128]{3,2,1,0:T(8,128)S(1)}, f32[2,4,32,128]{3,2,1,0:T(8,128)S(1)}, u32[]{:S(2)}, u32[]{:S(2)}) %collective-permute-start.5) | collective-permute-done | bytes 131104 | tf_op jit(solution)/shard_map/ppermute | solution.py:20
  81.5 3.7 %collective-permute-start.7 = (f32[2,40,4,128]{3,2,1,0:T(4,128)}, f32[2,40,4,128]{3,2,1,0:T(4,128)}, u32[]{:S(2)}, u32[]{:S(2)}) collective-permute-start(f32[2,40,4,128]{3,2,1,0:T(4,128)} %get-tuple-element.630), channel_id=1, source_target_pairs={{0,1},{1,2},{2,3},{3,4},{4,5},{5,6},{6,7},{8,9},{9,10},{10,11},{11... | collective-permute-start | bytes 491528 | tf_op jit(solution)/shard_map/ppermute | solution.py:20
  85.2 25.7 %while.61 = (s32[]{:T(128)}, f32[1024,128]{1,0:T(8,128)}, s32[8,512,3]{1,2,0:T(4,128)S(1)}, s32[]{:T(128)}, f32[8,512]{1,0:T(8,128)S(1)}, /*index=5*/s32[]{:T(128)}, s32[]{:T(128)}, s32[]{:T(128)}) while((s32[]{:T(128)}, f32[1024,128]{1,0:T(8,128)}, s32[8,512,3]{1,2,0:T(4,128)S(1)}, s32[]{:T(128)}, ...), condition=%wide.region_3.4_spmd.clone.clone, body=%wide.region_2.3_spmd.clone.clone.sunk | while | flops 806224896 | bytes 5541999 | solution.py:83
  87.8 3.0 %convolution_add_fusion.7 = f32[1024,128]{1,0:T(8,128)} fusion(f32[512,1024]{0,1:T(8,128)S(1)} %bitcast.148, f32[1024,128]{1,0:T(8,128)} %get-tuple-element.816, pred[]{:T(512)S(6)} %compare.92, s32[512]{0:T(512)S(1)} %bitcast.160), kind=kOutput, calls=%fused_computation.18.clone.1 | convolution fusion | flops 805634048 | bytes 3147777 | tf_op jit(solution)/shard_map/while/body/eval_jaxpr/dot_general | solution.py:73
  91.2 3.0 %convolution_add_fusion.7 = f32[1024,128]{1,0:T(8,128)} fusion(f32[512,1024]{0,1:T(8,128)S(1)} %bitcast.148, f32[1024,128]{1,0:T(8,128)} %get-tuple-element.816, pred[]{:T(512)S(6)} %compare.92, s32[512]{0:T(512)S(1)} %bitcast.160), kind=kOutput, calls=%fused_computation.18.clone.1 | convolution fusion | flops 805634048 | bytes 3147777 | tf_op jit(solution)/shard_map/while/body/eval_jaxpr/dot_general | solution.py:73
  94.5 3.0 %convolution_add_fusion.7 = f32[1024,128]{1,0:T(8,128)} fusion(f32[512,1024]{0,1:T(8,128)S(1)} %bitcast.148, f32[1024,128]{1,0:T(8,128)} %get-tuple-element.816, pred[]{:T(512)S(6)} %compare.92, s32[512]{0:T(512)S(1)} %bitcast.160), kind=kOutput, calls=%fused_computation.18.clone.1 | convolution fusion | flops 805634048 | bytes 3147777 | tf_op jit(solution)/shard_map/while/body/eval_jaxpr/dot_general | solution.py:73
  97.9 3.0 %convolution_add_fusion.7 = f32[1024,128]{1,0:T(8,128)} fusion(f32[512,1024]{0,1:T(8,128)S(1)} %bitcast.148, f32[1024,128]{1,0:T(8,128)} %get-tuple-element.816, pred[]{:T(512)S(6)} %compare.92, s32[512]{0:T(512)S(1)} %bitcast.160), kind=kOutput, calls=%fused_computation.18.clone.1 | convolution fusion | flops 805634048 | bytes 3147777 | tf_op jit(solution)/shard_map/while/body/eval_jaxpr/dot_general | solution.py:73
  101.2 3.0 %convolution_add_fusion.7 = f32[1024,128]{1,0:T(8,128)} fusion(f32[512,1024]{0,1:T(8,128)S(1)} %bitcast.148, f32[1024,128]{1,0:T(8,128)} %get-tuple-element.816, pred[]{:T(512)S(6)} %compare.92, s32[512]{0:T(512)S(1)} %bitcast.160), kind=kOutput, calls=%fused_computation.18.clone.1 | convolution fusion | flops 805634048 | bytes 3147777 | tf_op jit(solution)/shard_map/while/body/eval_jaxpr/dot_general | solution.py:73
  104.5 3.0 %convolution_add_fusion.7 = f32[1024,128]{1,0:T(8,128)} fusion(f32[512,1024]{0,1:T(8,128)S(1)} %bitcast.148, f32[1024,128]{1,0:T(8,128)} %get-tuple-element.816, pred[]{:T(512)S(6)} %compare.92, s32[512]{0:T(512)S(1)} %bitcast.160), kind=kOutput, calls=%fused_computation.18.clone.1 | convolution fusion | flops 805634048 | bytes 3147777 | tf_op jit(solution)/shard_map/while/body/eval_jaxpr/dot_general | solution.py:73
  107.9 3.0 %convolution_add_fusion.7 = f32[1024,128]{1,0:T(8,128)} fusion(f32[512,1024]{0,1:T(8,128)S(1)} %bitcast.148, f32[1024,128]{1,0:T(8,128)} %get-tuple-element.816, pred[]{:T(512)S(6)} %compare.92, s32[512]{0:T(512)S(1)} %bitcast.160), kind=kOutput, calls=%fused_computation.18.clone.1 | convolution fusion | flops 805634048 | bytes 3147777 | tf_op jit(solution)/shard_map/while/body/eval_jaxpr/dot_general | solution.py:73
  115.3 3.2 %select_maximum_fusion.4 = f32[2,40,40,136]{3,2,1,0:T(8,128)S(1)} fusion(f32[2,40,4,128]{3,2,1,0:T(4,128)} %collective-permute-done.6, f32[2,40,4,128]{3,2,1,0:T(4,128)} %collective-permute-done.7, f32[2,4,32,128]{3,2,1,0:T(8,128)S(1)} %collective-permute-done.4, f32[2,32,32,128]{3,2,1,0:T(8,128)S(1)} %fusion.114, ...), kind=kLoop, calls=%fused_computation.48 | loop fusion | flops 5222400 | bytes 3379200 | tf_op jit(solution)/shard_map/concatenate | solution.py:24
  118.5 6.3 %multiply_add_fusion.1 = (f32[2,32,32,128]{3,2,1,0:T(8,128)}, f32[2,32,32,128]{3,2,1,0:T(8,128)}) fusion(f32[2,32,32,128]{3,2,1,0:T(8,128)S(1)} %copy-done.1, f32[2,32,32,128]{3,2,1,0:T(8,128)S(1)} %fusion.114, f32[32,32,128]{2,1,0:T(8,128)S(1)} %copy-done.7, f32[2,40,40,136]{3,2,1,0:T(8,128)S(1)} %select_maximum_fusion.4, ...), kind=kLoop, calls=%fused_computation.218 | loop fusion | flops 10747904 | bytes 21757952 | tf_op jit(solution)/shard_map/add | solution.py:119
  130.7 3.9 %collective-permute-start.9 = (f32[2,4,32,128]{3,2,1,0:T(8,128)S(1)}, f32[2,4,32,128]{3,2,1,0:T(8,128)S(1)}, u32[]{:S(2)}, u32[]{:S(2)}) collective-permute-start(f32[2,4,32,128]{3,2,1,0:T(8,128)S(1)} %get-tuple-element.636), channel_id=1, source_target_pairs={{0,8},{8,16},{16,24},{24,32},{32,40},{40,48},{48,56},{56,64},{64,7... | collective-permute-start | bytes 393224 | tf_op jit(solution)/shard_map/ppermute | solution.py:20
  141.0 3.7 %collective-permute-start.11 = (f32[2,40,4,128]{3,2,1,0:T(4,128)}, f32[2,40,4,128]{3,2,1,0:T(4,128)}, u32[]{:S(2)}, u32[]{:S(2)}) collective-permute-start(f32[2,40,4,128]{3,2,1,0:T(4,128)} %get-tuple-element.626), channel_id=1, source_target_pairs={{0,1},{1,2},{2,3},{3,4},{4,5},{5,6},{6,7},{8,9},{9,10},{10,11},{11... | collective-permute-start | bytes 491528 | tf_op jit(solution)/shard_map/ppermute | solution.py:20
  148.3 3.1 %select_maximum_fusion = f32[2,40,40,136]{3,2,1,0:T(8,128)S(1)} fusion(f32[2,40,4,128]{3,2,1,0:T(4,128)} %collective-permute-done.10, f32[2,40,4,128]{3,2,1,0:T(4,128)} %collective-permute-done.11, f32[2,4,32,128]{3,2,1,0:T(8,128)S(1)} %collective-permute-done.8, f32[2,32,32,128]{3,2,1,0:T(8,128)S(1)} %fusion.115, ...), kind=kLoop, calls=%fused_computation.44 | loop fusion | flops 5222400 | bytes 3379200 | tf_op jit(solution)/shard_map/concatenate | solution.py:24
  151.5 7.4 %multiply_add_fusion = (f32[2,32,32,128]{3,2,1,0:T(8,128)}, f32[2,32,32,128]{3,2,1,0:T(8,128)}) fusion(f32[2,32,32,128]{3,2,1,0:T(8,128)S(1)} %fusion.114, f32[2,32,32,128]{3,2,1,0:T(8,128)S(1)} %fusion.115, f32[32,32,128]{2,1,0:T(8,128)S(1)} %copy-done.8, f32[2,40,40,136]{3,2,1,0:T(8,128)S(1)} %select_maximum_fusion, ...), kind=kLoop, calls=%fused_computation.217 | loop fusion | flops 10747904 | bytes 21757952 | tf_op jit(solution)/shard_map/add | solution.py:119
  158.9 3.3 %fusion.107 = f32[32,32,128]{2,1,0:T(8,128)} fusion(f32[2,32,32,128]{3,2,1,0:T(8,128)} %get-tuple-element.610, f32[2,32,32,128]{3,2,1,0:T(8,128)} %get-tuple-element.612, f32[2,32,32,128]{3,2,1,0:T(8,128)} %get-tuple-element.614, f32[1,32,32,128]{3,2,1,0:T(8,128)} %param.29, f32[32,32,128]{2,1,0:T(8,128)} %param.31, f32[1,32,32,128]{3,2,1,0:T(8,128)S(1)} %bitcast.151, ...), kind=kLoop, calls=%fused_computation.221 | loop fusion | flops 1441792 | bytes 5242880 | tf_op jit(solution)/shard_map/add | solution.py:88
  162.3 14.0 %while.62 = (s32[]{:T(128)}, f32[1024,128]{1,0:T(8,128)S(1)}, s32[8,512,3]{1,2,0:T(4,128)S(1)}, s32[]{:T(128)}, f32[8,512]{1,0:T(8,128)S(1)}, /*index=5*/s32[]{:T(128)}, s32[]{:T(128)}, s32[]{:T(128)}) while((s32[]{:T(128)}, f32[1024,128]{1,0:T(8,128)S(1)}, s32[8,512,3]{1,2,0:T(4,128)S(1)}, s32[]{:T(128)}, ...), condition=%wide.region_5.6_spmd.clone.clone, body=%wide.region_4.5_spmd.clone.clone.sunk | while | flops 806224896 | bytes 5541999 | solution.py:83
  180.0 75.2 %all-reduce.5.cloned.1.call-done = f32[32,32,128]{2,1,0:T(8,128)} async-done(((f32[32,32,128]{2,1,0:T(8,128)}), f32[32,32,128]{2,1,0:T(8,128)}) %all-reduce.5.cloned.1.call-update) | async-done | bytes 524304 | tf_op jit(solution)/shard_map/psum | solution.py:124
  (262 shorter events, 68.7 us)
Async XLA Ops:
  7.2 12.7 %copy-start.9 = (f32[32,32,128]{2,1,0:T(8,128)S(1)}, f32[32,32,128]{2,1,0:T(8,128)}, u32[]{:S(2)}) copy-start(f32[32,32,128]{2,1,0:T(8,128)} %param.31) | copy-start | bytes 1572868
  7.2 13.6 %copy-start.22 = (s32[1,16,3]{1,0,2:T(1,128)S(1)}, s32[1,16,3]{1,0,2:T(1,128)}, u32[]{:S(2)}) copy-start(s32[1,16,3]{1,0,2:T(1,128)} %param.32) | copy-start | bytes 580
  7.2 13.6 %copy-start.23 = (f32[1,3,16]{2,0,1:T(1,128)S(1)}, f32[1,3,16]{2,0,1:T(1,128)}, u32[]{:S(2)}) copy-start(f32[1,3,16]{2,0,1:T(1,128)} %param.33) | copy-start | bytes 580
  7.2 13.6 %copy-start.18 = (f32[1,3,4096]{2,0,1:T(1,128)S(1)}, f32[1,3,4096]{2,0,1:T(1,128)}, u32[]{:S(2)}) copy-start(f32[1,3,4096]{2,0,1:T(1,128)} %param.35) | copy-start | bytes 147460
  7.2 14.3 %copy-start.17 = (s32[1,4096,3]{1,0,2:T(1,128)S(1)}, s32[1,4096,3]{1,0,2:T(1,128)}, u32[]{:S(2)}) copy-start(s32[1,4096,3]{1,0,2:T(1,128)} %param.34) | copy-start | bytes 147460
  7.2 248.0 %all-reduce.5.cloned.1.call-start = ((), (), s32[]{:S(2)}) async-start(), calls=%async_computation | async-start | bytes 1048576 | tf_op jit(solution)/shard_map/psum | solution.py:124
  9.5 51.0 %copy-start = (f32[2,32,32,128]{3,2,1,0:T(8,128)}, f32[2,32,32,128]{3,2,1,0:T(8,128)S(1)}, u32[]{:S(2)}) copy-start(f32[2,32,32,128]{3,2,1,0:T(8,128)S(1)} %constant_dynamic-update-slice_fusion) | copy-start | bytes 3145732
  10.3 37.9 %collective-permute-start = (f32[2,4,32,128]{3,2,1,0:T(8,128)}, f32[2,4,32,128]{3,2,1,0:T(8,128)S(1)}, u32[]{:S(2)}, u32[]{:S(2)}) collective-permute-start(f32[2,4,32,128]{3,2,1,0:T(8,128)} %get-tuple-element.641), channel_id=1, source_target_pairs={{8,0},{16,8},{24,16},{32,24},{40,32},{48,40},{56,48},{64,56},{72,6... | collective-permute-start | bytes 393224 | tf_op jit(solution)/shard_map/ppermute | solution.py:23
  18.0 30.2 %collective-permute-start.1 = (f32[2,4,32,128]{3,2,1,0:T(8,128)}, f32[2,4,32,128]{3,2,1,0:T(8,128)S(1)}, u32[]{:S(2)}, u32[]{:S(2)}) collective-permute-start(f32[2,4,32,128]{3,2,1,0:T(8,128)} %get-tuple-element.640), channel_id=1, source_target_pairs={{0,8},{8,16},{16,24},{24,32},{32,40},{40,48},{48,56},{56,64},{64,7... | collective-permute-start | bytes 393224 | tf_op jit(solution)/shard_map/ppermute | solution.py:20
  48.2 6.4 %collective-permute-start.2 = (f32[2,40,4,128]{3,2,1,0:T(4,128)S(1)}, f32[2,40,4,128]{3,2,1,0:T(4,128)S(1)}, u32[]{:S(2)}, u32[]{:S(2)}) collective-permute-start(f32[2,40,4,128]{3,2,1,0:T(4,128)S(1)} %get-tuple-element.635), channel_id=1, source_target_pairs={{1,0},{2,1},{3,2},{4,3},{5,4},{6,5},{7,6},{9,8},{10,9},{11,10},{12... | collective-permute-start | bytes 491528 | tf_op jit(solution)/shard_map/ppermute | solution.py:23
  49.5 5.1 %collective-permute-start.3 = (f32[2,40,4,128]{3,2,1,0:T(4,128)S(1)}, f32[2,40,4,128]{3,2,1,0:T(4,128)S(1)}, u32[]{:S(2)}, u32[]{:S(2)}) collective-permute-start(f32[2,40,4,128]{3,2,1,0:T(4,128)S(1)} %get-tuple-element.634), channel_id=1, source_target_pairs={{0,1},{1,2},{2,3},{3,4},{4,5},{5,6},{6,7},{8,9},{9,10},{10,11},{11... | collective-permute-start | bytes 491528 | tf_op jit(solution)/shard_map/ppermute | solution.py:20
  57.4 3.1 %copy-start.6 = (f32[32,32,128]{2,1,0:T(8,128)S(1)}, f32[32,32,128]{2,1,0:T(8,128)}, u32[]{:S(2)}) copy-start(f32[32,32,128]{2,1,0:T(8,128)} %mul.262) | copy-start | bytes 1572868
  60.5 6.2 %copy-start.12 = (f32[32,32,16]{1,0,2:T(8,128)S(1)}, f32[32,32,16]{1,0,2:T(8,128)}, u32[]{:S(2)}) copy-start(f32[32,32,16]{1,0,2:T(8,128)} %reshape.680) | copy-start | bytes 196612
  60.5 6.2 %copy-start.19 = (s32[16]{0:T(128)S(1)}, s32[16]{0:T(128)}, u32[]{:S(2)}) copy-start(s32[16]{0:T(128)} %get-tuple-element.645) | copy-start | bytes 196
  67.5 6.8 %copy-start.16 = (f32[4096]{0:T(1024)S(1)}, f32[4096]{0:T(1024)}, u32[]{:S(2)}) copy-start(f32[4096]{0:T(1024)} %get-tuple-element.572) | copy-start | bytes 49156
  68.5 7.3 %collective-permute-start.4 = (f32[2,4,32,128]{3,2,1,0:T(8,128)S(1)}, f32[2,4,32,128]{3,2,1,0:T(8,128)S(1)}, u32[]{:S(2)}, u32[]{:S(2)}) collective-permute-start(f32[2,4,32,128]{3,2,1,0:T(8,128)S(1)} %get-tuple-element.639), channel_id=1, source_target_pairs={{8,0},{16,8},{24,16},{32,24},{40,32},{48,40},{56,48},{64,56},{72,6... | collective-permute-start | bytes 393224 | tf_op jit(solution)/shard_map/ppermute | solution.py:23
  72.4 7.0 %collective-permute-start.5 = (f32[2,4,32,128]{3,2,1,0:T(8,128)S(1)}, f32[2,4,32,128]{3,2,1,0:T(8,128)S(1)}, u32[]{:S(2)}, u32[]{:S(2)}) collective-permute-start(f32[2,4,32,128]{3,2,1,0:T(8,128)S(1)} %get-tuple-element.638), channel_id=1, source_target_pairs={{0,8},{8,16},{16,24},{24,32},{32,40},{40,48},{48,56},{56,64},{64,7... | collective-permute-start | bytes 393224 | tf_op jit(solution)/shard_map/ppermute | solution.py:20
  80.2 32.6 %collective-permute-start.6 = (f32[2,40,4,128]{3,2,1,0:T(4,128)}, f32[2,40,4,128]{3,2,1,0:T(4,128)}, u32[]{:S(2)}, u32[]{:S(2)}) collective-permute-start(f32[2,40,4,128]{3,2,1,0:T(4,128)} %get-tuple-element.631), channel_id=1, source_target_pairs={{1,0},{2,1},{3,2},{4,3},{5,4},{6,5},{7,6},{9,8},{10,9},{11,10},{12... | collective-permute-start | bytes 491528 | tf_op jit(solution)/shard_map/ppermute | solution.py:23
  81.5 31.3 %collective-permute-start.7 = (f32[2,40,4,128]{3,2,1,0:T(4,128)}, f32[2,40,4,128]{3,2,1,0:T(4,128)}, u32[]{:S(2)}, u32[]{:S(2)}) collective-permute-start(f32[2,40,4,128]{3,2,1,0:T(4,128)} %get-tuple-element.630), channel_id=1, source_target_pairs={{0,1},{1,2},{2,3},{3,4},{4,5},{5,6},{6,7},{8,9},{9,10},{10,11},{11... | collective-permute-start | bytes 491528 | tf_op jit(solution)/shard_map/ppermute | solution.py:20
  115.3 3.2 %copy-start.1 = (f32[2,32,32,128]{3,2,1,0:T(8,128)S(1)}, f32[2,32,32,128]{3,2,1,0:T(8,128)}, u32[]{:S(2)}) copy-start(f32[2,32,32,128]{3,2,1,0:T(8,128)} %copy-done) | copy-start | bytes 3145732
  115.3 3.2 %copy-start.7 = (f32[32,32,128]{2,1,0:T(8,128)S(1)}, f32[32,32,128]{2,1,0:T(8,128)}, u32[]{:S(2)}) copy-start(f32[32,32,128]{2,1,0:T(8,128)} %mul.262) | copy-start | bytes 1572868
  118.5 6.3 %copy-start.13 = (f32[32,32,16]{1,0,2:T(8,128)S(1)}, f32[32,32,16]{1,0,2:T(8,128)}, u32[]{:S(2)}) copy-start(f32[32,32,16]{1,0,2:T(8,128)} %reshape.682) | copy-start | bytes 196612
  118.5 6.3 %copy-start.20 = (s32[16]{0:T(128)S(1)}, s32[16]{0:T(128)}, u32[]{:S(2)}) copy-start(s32[16]{0:T(128)} %get-tuple-element.645) | copy-start | bytes 196
  124.8 3.8 %copy-start.4 = (f32[1024,128]{1,0:T(8,128)S(1)}, f32[1024,128]{1,0:T(8,128)}, u32[]{:S(2)}) copy-start(f32[1024,128]{1,0:T(8,128)} %get-tuple-element.415) | copy-start | bytes 1572868
  128.8 7.5 %collective-permute-start.8 = (f32[2,4,32,128]{3,2,1,0:T(8,128)S(1)}, f32[2,4,32,128]{3,2,1,0:T(8,128)S(1)}, u32[]{:S(2)}, u32[]{:S(2)}) collective-permute-start(f32[2,4,32,128]{3,2,1,0:T(8,128)S(1)} %get-tuple-element.637), channel_id=1, source_target_pairs={{8,0},{16,8},{24,16},{32,24},{40,32},{48,40},{56,48},{64,56},{72,6... | collective-permute-start | bytes 393224 | tf_op jit(solution)/shard_map/ppermute | solution.py:23
  130.7 8.2 %collective-permute-start.9 = (f32[2,4,32,128]{3,2,1,0:T(8,128)S(1)}, f32[2,4,32,128]{3,2,1,0:T(8,128)S(1)}, u32[]{:S(2)}, u32[]{:S(2)}) collective-permute-start(f32[2,4,32,128]{3,2,1,0:T(8,128)S(1)} %get-tuple-element.636), channel_id=1, source_target_pairs={{0,8},{8,16},{16,24},{24,32},{32,40},{40,48},{48,56},{56,64},{64,7... | collective-permute-start | bytes 393224 | tf_op jit(solution)/shard_map/ppermute | solution.py:20
  139.7 5.0 %collective-permute-start.10 = (f32[2,40,4,128]{3,2,1,0:T(4,128)}, f32[2,40,4,128]{3,2,1,0:T(4,128)}, u32[]{:S(2)}, u32[]{:S(2)}) collective-permute-start(f32[2,40,4,128]{3,2,1,0:T(4,128)} %get-tuple-element.627), channel_id=1, source_target_pairs={{1,0},{2,1},{3,2},{4,3},{5,4},{6,5},{7,6},{9,8},{10,9},{11,10},{12... | collective-permute-start | bytes 491528 | tf_op jit(solution)/shard_map/ppermute | solution.py:23
  141.0 4.4 %collective-permute-start.11 = (f32[2,40,4,128]{3,2,1,0:T(4,128)}, f32[2,40,4,128]{3,2,1,0:T(4,128)}, u32[]{:S(2)}, u32[]{:S(2)}) collective-permute-start(f32[2,40,4,128]{3,2,1,0:T(4,128)} %get-tuple-element.626), channel_id=1, source_target_pairs={{0,1},{1,2},{2,3},{3,4},{4,5},{5,6},{6,7},{8,9},{9,10},{10,11},{11... | collective-permute-start | bytes 491528 | tf_op jit(solution)/shard_map/ppermute | solution.py:20
  148.3 3.1 %copy-start.8 = (f32[32,32,128]{2,1,0:T(8,128)S(1)}, f32[32,32,128]{2,1,0:T(8,128)}, u32[]{:S(2)}) copy-start(f32[32,32,128]{2,1,0:T(8,128)} %mul.262) | copy-start | bytes 1572868
  151.5 7.4 %copy-start.3 = (f32[1024,128]{1,0:T(8,128)S(1)}, f32[1024,128]{1,0:T(8,128)}, u32[]{:S(2)}) copy-start(f32[1024,128]{1,0:T(8,128)} %get-tuple-element.414) | copy-start | bytes 1572868
  162.3 14.0 %copy-start.11 = (f32[16,32,32]{2,1,0:T(8,128)S(1)}, f32[16,32,32]{2,1,0:T(8,128)}, u32[]{:S(2)}) copy-start(f32[16,32,32]{2,1,0:T(8,128)} %get-tuple-element.642) | copy-start | bytes 196612
  162.3 14.3 %copy-start.21 = (s32[16]{0:T(128)S(1)}, s32[16]{0:T(128)}, u32[]{:S(2)}) copy-start(s32[16]{0:T(128)} %get-tuple-element.645) | copy-start | bytes 196
  (5 other events, 6.2 us)
Sparse Core Ops, SparseCore 0:
  162.4 92.7 all-reduce.4
where the time goes:
time: 265 us; the launch traced here: 264 us
  waiting for transfers between devices  85.3 us (32%)
  matrix products  62.9 us (24%)
  other arithmetic  53.8 us (20%)
  starting transfers between devices  35.6 us (13%)
  between operations  14.5 us (5%)
  local copies, waits for them, and re-layouts  10.7 us (4%)
    psum x1, waiting for transfers between devices, shards(): gradient = lax.psum(summed, 'shot')  75.2 us
    dot_general x27, matrix products, one_block(): lax.dot_general(plane, hit_z, (((0,), (0,)), ((), ())), precision=lax.Pre...  62.9 us
    add x3, other arithmetic, shards(): earlier = 2.0 * current - later + squared * curved  19.9 us
    ppermute x6, starting transfers between devices, extended_2(): lax.ppermute(lax.slice_in_dim(block, block.shape[dim] - width, None, axis...  18.2 us
    concatenate x9, other arithmetic, extended_2(): block = jnp.concatenate([low, block, high], axis=dim)  17.9 us
    ppermute x6, starting transfers between devices, extended_2(): lax.ppermute(lax.slice_in_dim(block, 0, width, axis=dim), axis, backward)  17.4 us
    mul x25, other arithmetic, one_block(): hit_x[:, :, None] * hit_y[:, None, :]  7.21 us
    ppermute x6, waiting for transfers between devices, extended_2(): lax.ppermute(lax.slice_in_dim(block, block.shape[dim] - width, None, axis...  7.05 us
  transfers between devices with their start and end apart: 13, of which 6 were waited for; matrix products, arithmetic and copies ran while one was open for 28% of the time, Pallas kernels for 0%

commit v1 on v0

v1 whole, which is shorter than its diff:
```python
import functools

import jax
import jax.numpy as jnp
from jax import lax
from jax.experimental import pallas as pl
from jax.experimental.pallas import tpu as pltpu
from jax.sharding import PartitionSpec as P

STEPS = 3
W = 4
PADY = 8
SLOTS = 256
LANES = 128
COEFFS = (-205.0 / 72.0, 8.0 / 5.0, -1.0 / 5.0, 8.0 / 315.0, -1.0 / 560.0)
GRAD_SCALE = 0.1
MESH = pl.DeviceIdType.MESH
VMEM_LIMIT = 48 * 1024 * 1024


def scatter_kernel(rows_x, rows_y, chunks, feats_ref, mask_ref, sfeats_ref, out_p, out_q, rank_ref):
    cells = rows_x * rows_y
    f32, bf16 = jnp.float32, jnp.bfloat16
    nt = (((1,), (1,)), ((), ()))

    def spread(by_row, by_col, out, add):
        slots = by_row.shape[1]
        place = by_row[0:1, :] * float(rows_y) + by_row[1:2, :]
        ids = lax.broadcasted_iota(jnp.int32, (cells, slots), 0).astype(f32)
        left = (ids == place).astype(f32).astype(bf16)
        lane = lax.broadcasted_iota(jnp.int32, (slots, LANES), 1).astype(f32)
        hit = lane == by_col[:, 2:3]
        for step in range(STEPS):
            high = jnp.where(hit, by_col[:, 3 + step : 4 + step], 0.0)
            low = jnp.where(hit, by_col[:, 6 + step : 7 + step], 0.0)
            right = jnp.concatenate([high, low], axis=1).astype(bf16)
            both = jnp.dot(left, right, preferred_element_type=f32)
            total = (both[:, :LANES] + both[:, LANES:]).reshape(rows_x, rows_y, LANES)
            if add:
                out[step] = out[step] + total
            else:
                out[step] = total

    sfeats = sfeats_ref[...]
    inside = (
        (sfeats[0:1] >= 0.0)
        & (sfeats[0:1] < float(rows_x))
        & (sfeats[1:2] >= 0.0)
        & (sfeats[1:2] < float(rows_y))
    )
    sfeats = jnp.where(inside, sfeats, 0.0)
    spread(sfeats, sfeats.T, out_p, False)

    mask = mask_ref[...]
    ones = mask.astype(bf16)
    row = lax.broadcasted_iota(jnp.int32, (LANES, LANES), 0)
    col = lax.broadcasted_iota(jnp.int32, (LANES, LANES), 1)
    upper = (row <= col).astype(f32).astype(bf16)
    inclusive = jnp.dot(ones, upper, preferred_element_type=f32)
    totals = jnp.broadcast_to(inclusive[:, LANES - 1 : LANES], (chunks, LANES)).astype(bf16)
    crow = lax.broadcasted_iota(jnp.int32, (chunks, chunks), 0)
    ccol = lax.broadcasted_iota(jnp.int32, (chunks, chunks), 1)
    before = (ccol < crow).astype(f32).astype(bf16)
    offsets = jnp.dot(before, totals, preferred_element_type=f32)
    rank_ref[...] = jnp.where(mask > 0.5, offsets + inclusive - 1.0, -1.0)
    count = jnp.sum(mask).astype(jnp.int32)
    out_q[...] = jnp.zeros_like(out_q)

    def one_round(turn, carry):
        slot = lax.broadcasted_iota(jnp.int32, (SLOTS, LANES), 0).astype(f32)
        base = (turn * SLOTS).astype(f32)
        by_row = jnp.zeros((16, SLOTS), f32)
        by_col = jnp.zeros((SLOTS, 16), f32)
        for chunk in range(chunks):
            rank = rank_ref[chunk : chunk + 1, :] - base
            pick = (slot == rank).astype(f32).astype(bf16)
            part = feats_ref[:, chunk * LANES : (chunk + 1) * LANES].astype(bf16)
            by_row = by_row + lax.dot_general(part, pick, nt, preferred_element_type=f32)
            by_col = by_col + lax.dot_general(pick, part, nt, preferred_element_type=f32)
        spread(by_row, by_col, out_q, True)
        return carry

    lax.fori_loop(0, (count + SLOTS - 1) // SLOTS, one_round, 0)


def features(cells, values, start_x, start_y):
    count = cells.shape[0]
    high = lax.reduce_precision(values, 8, 7)
    local = cells.T - jnp.stack([start_x, start_y, jnp.int32(0)])[:, None]
    rows = [local.astype(jnp.float32), high, values - high, jnp.zeros((7, count), jnp.float32)]
    padded = -(-count // LANES) * LANES
    if padded == count:
        return jnp.concatenate(rows, 0)
    rows = jnp.concatenate(rows, 0)
    tail = jnp.full((16, padded - count), -1.0, jnp.float32)
    return jnp.concatenate([rows, tail], 1)


def wave_kernel(
    sizes, p0, p2, q0, q2, courant, add_p, add_q, out_p, out_q, out_g,
    ext, last, cour, adds, final, gacc, gout, rbuf, ysend, yrecv,
    load_sem, xs, xr, ys, yr, gs, gr, hs, hr, store_sem,
):
    n_shot, n_gx, n_gy, rx, ry = sizes
    me_s = lax.axis_index("shot")
    me_x = lax.axis_index("gx")
    me_y = lax.axis_index("gy")
    fields = (p0, q0)
    mid_x = pl.ds(W, rx)
    mid_y = pl.ds(PADY, ry)
    part = rx // n_shot

    loads = []

    def load(src, dst):
        copy = pltpu.make_async_copy(src, dst, load_sem.at[len(loads)])
        copy.start()
        loads.append(copy)

    load(p0, ext.at[0, 0, mid_x, mid_y])
    load(q0, ext.at[0, 1, mid_x, mid_y])
    load(courant, cour)
    load(p2, last.at[0])
    load(q2, last.at[1])
    load(add_p, adds.at[0])
    load(add_q, adds.at[1])

    for step in range(STEPS):
        for f in range(2):
            zx = jnp.zeros((W, ry, LANES), jnp.float32)
            zy = jnp.zeros((rx, W, LANES), jnp.float32)

            @pl.when(me_x == 0)
            def _():
                ext[step, f, 0:W, PADY : PADY + ry, :] = zx

            @pl.when(me_x == n_gx - 1)
            def _():
                ext[step, f, W + rx : 2 * W + rx, PADY : PADY + ry, :] = zx

            @pl.when(me_y == 0)
            def _():
                yrecv[step, f, 0] = zy

            @pl.when(me_y == n_gy - 1)
            def _():
                yrecv[step, f, 1] = zy

    barrier = pltpu.get_barrier_semaphore()
    has = (me_x < n_gx - 1, me_x > 0, me_y < n_gy - 1, me_y > 0)
    up_x = jnp.minimum(me_x + 1, n_gx - 1)
    down_x = jnp.maximum(me_x - 1, 0)
    up_y = jnp.minimum(me_y + 1, n_gy - 1)
    down_y = jnp.maximum(me_y - 1, 0)
    ids = ({"gx": up_x}, {"gx": down_x}, {"gy": up_y}, {"gy": down_y})
    for k in range(4):

        @pl.when(has[k])
        def _():
            pl.semaphore_signal(barrier, inc=1, device_id=ids[k], device_id_type=MESH)

    peers = [lax.rem(me_s + d, n_shot) for d in range(1, n_shot)]
    for peer in peers:
        pl.semaphore_signal(barrier, inc=1, device_id={"shot": peer}, device_id_type=MESH)
    expected = n_shot - 1
    for k in range(4):
        expected = expected + has[k].astype(jnp.int32)
    pl.semaphore_wait(barrier, expected)

    def x_copy(step, f, side):
        first = (rx - W) if side == 0 else 0
        if step == 0:
            src = fields[f].at[pl.ds(first, W)]
        else:
            src = ext.at[step, f, pl.ds(W + first, W), mid_y]
        dst = ext.at[step, f, pl.ds(0 if side == 0 else W + rx, W), mid_y]
        return pltpu.make_async_remote_copy(
            src_ref=src, dst_ref=dst, send_sem=xs.at[step, f, side], recv_sem=xr.at[step, f, side],
            device_id=ids[side], device_id_type=MESH,
        )

    def y_copy(step, f, side):
        return pltpu.make_async_remote_copy(
            src_ref=ysend.at[step, f, side], dst_ref=yrecv.at[step, f, side],
            send_sem=ys.at[step, f, side], recv_sem=yr.at[step, f, side],
            device_id=ids[2 + side], device_id_type=MESH,
        )

    def start_x(step, f):
        for side in range(2):

            @pl.when(has[side])
            def _():
                x_copy(step, f, side).start()

    def start_y(step, f):
        ysend[step, f, 0] = ext[step, f, W : W + rx, PADY + ry - W : PADY + ry, :]
        ysend[step, f, 1] = ext[step, f, W : W + rx, PADY : PADY + W, :]
        for side in range(2):

            @pl.when(has[2 + side])
            def _():
                y_copy(step, f, side).start()

    def wait_x(step, f):
        for side in range(2):

            @pl.when(has[1 - side])
            def _():
                x_copy(step, f, side).wait_recv()

    def wait_y(step, f):
        for side in range(2):

            @pl.when(has[3 - side])
            def _():
                y_copy(step, f, side).wait_recv()

        ext[step, f, W : W + rx, PADY - W : PADY, :] = yrecv[step, f, 0]
        ext[step, f, W : W + rx, PADY + ry : PADY + ry + W, :] = yrecv[step, f, 1]

    lane = lax.broadcasted_iota(jnp.int32, (ry, LANES), 1)

    def plane(step, f, x):
        here = ext[step, f, x + W, PADY : PADY + ry, :]
        total = (3.0 * COEFFS[0]) * here
        for k in range(1, W + 1):
            pairs = (
                ext[step, f, x + W + k, PADY : PADY + ry, :] + ext[step, f, x + W - k, PADY : PADY + ry, :]
            ) + (
                ext[step, f, x + W, PADY + k : PADY + ry + k, :]
                + ext[step, f, x + W, PADY - k : PADY + ry - k, :]
            )
            right = jnp.where(lane < LANES - k, pltpu.roll(here, LANES - k, 1), 0.0)
            left = jnp.where(lane >= k, pltpu.roll(here, k, 1), 0.0)
            total = total + COEFFS[k] * (pairs + (right + left))
        return here, total

    def previous(step, f, x):
        if step == 0:
            return last[f, x]
        return ext[step - 1, f, x + W, PADY : PADY + ry, :]

    def advance(step, f, x):
        here, curved = plane(step, f, x)
        if f == 0:
            term = ext[step, 1, x + W, PADY : PADY + ry, :] * curved
            gacc[x] = term if step == 0 else gacc[x] + term
        speed = cour[x]
        fresh = 2.0 * here - previous(step, f, x) + (speed * speed) * curved + adds[f, step, x]
        if step < STEPS - 1:
            ext[step + 1, f, x + W, PADY : PADY + ry, :] = fresh
        else:
            final[f, x] = fresh

    def planes(step, f, low, high):
        def body(x, carry):
            advance(step, f, x)
            return carry

        lax.fori_loop(low, high, body, 0)

    for f in range(2):
        start_x(0, f)
    loads[0].wait()
    start_y(0, 0)
    loads[1].wait()
    start_y(0, 1)
    for copy in loads[2:]:
        copy.wait()
    stores = []
    reduce_sends = []
    for step in range(STEPS):
        for f in range(2):
            wait_y(step, f)
            planes(step, f, W, rx - W)
        for f in range(2):
            wait_x(step, f)
            planes(step, f, 0, W)
            planes(step, f, rx - W, rx)
            if step < STEPS - 1:
                start_x(step + 1, f)
                start_y(step + 1, f)
            else:
                copy = pltpu.make_async_copy(final.at[f], (out_p, out_q)[f], store_sem.at[f])
                copy.start()
                stores.append(copy)
            if step == STEPS - 1 and f == 0:
                for d, peer in enumerate(peers):
                    copy = pltpu.make_async_remote_copy(
                        src_ref=gacc.at[pl.ds(peer * part, part)], dst_ref=rbuf.at[d],
                        send_sem=gs.at[d], recv_sem=gr.at[d],
                        device_id={"shot": peer}, device_id_type=MESH,
                    )
                    copy.start()
                    reduce_sends.append(copy)

    for copy in reduce_sends:
        copy.wait_recv()
    mine = pl.ds(me_s * part, part)
    total = gacc[mine]
    for d in range(n_shot - 1):
        total = total + rbuf[d]
    gout[mine] = total * ((2.0 * GRAD_SCALE) * cour[mine])
    gathers = []
    for d, peer in enumerate(peers):
        copy = pltpu.make_async_remote_copy(
            src_ref=gout.at[mine], dst_ref=gout.at[mine], send_sem=hs.at[d], recv_sem=hr.at[d],
            device_id={"shot": peer}, device_id_type=MESH,
        )
        copy.start()
        gathers.append(copy)
    for d, copy in enumerate(gathers):
        other = lax.rem(me_s + n_shot - 1 - d, n_shot)
        theirs = gout.at[pl.ds(other * part, part)]
        pltpu.make_async_remote_copy(
            src_ref=theirs, dst_ref=theirs, send_sem=hs.at[d], recv_sem=hr.at[d],
            device_id={"shot": other}, device_id_type=MESH,
        ).wait_recv()
    copy = pltpu.make_async_copy(gout, out_g, store_sem.at[2])
    copy.start()
    stores.append(copy)
    for step in range(STEPS):
        for f in range(2):
            for side in range(2):

                @pl.when(has[side])
                def _():
                    x_copy(step, f, side).wait_send()

                @pl.when(has[2 + side])
                def _():
                    y_copy(step, f, side).wait_send()

    for copy in reduce_sends + gathers:
        copy.wait_send()
    for copy in stores:
        copy.wait()


def shards(
    mesh_sizes, forward_now, forward_later, adjoint_now, adjoint_later, courant,
    source_cells, source_wave, receiver_cells, residual,
):
    rx, ry, depth = courant.shape
    n_shot, n_gx, n_gy = mesh_sizes
    f32 = jnp.float32
    start_x = (lax.axis_index("gx") * rx).astype(jnp.int32)
    start_y = (lax.axis_index("gy") * ry).astype(jnp.int32)
    feats = features(receiver_cells[0], residual[0], start_x, start_y)
    sfeats = features(source_cells[0], source_wave[0], start_x, start_y)
    mask = (feats[0] >= 0) & (feats[0] < rx) & (feats[1] >= 0) & (feats[1] < ry)
    chunks = feats.shape[1] // LANES
    mask = mask.astype(f32).reshape(chunks, LANES)
    whole = pl.BlockSpec(memory_space=pltpu.VMEM)
    anywhere = pl.BlockSpec(memory_space=pl.ANY)
    block = jax.ShapeDtypeStruct((rx, ry, depth), f32)
    added = jax.ShapeDtypeStruct((STEPS, rx, ry, depth), f32)
    add_p, add_q = pl.pallas_call(
        functools.partial(scatter_kernel, rx, ry, chunks),
        out_shape=(added, added),
        in_specs=[whole] * 3,
        out_specs=(whole, whole),
        scratch_shapes=[pltpu.VMEM((chunks, LANES), f32)],
        compiler_params=pltpu.CompilerParams(vmem_limit_bytes=VMEM_LIMIT),
        name="scatter",
    )(feats, mask, sfeats)
    sizes = (n_shot, n_gx, n_gy, rx, ry)
    dma = pltpu.SemaphoreType.DMA
    out_p, out_q, out_g = pl.pallas_call(
        functools.partial(wave_kernel, sizes),
        out_shape=(block, block, block),
        in_specs=[anywhere] * 7,
        out_specs=(anywhere,) * 3,
        scratch_shapes=[
            pltpu.VMEM((STEPS, 2, rx + 2 * W, ry + 2 * PADY, depth), f32),
            pltpu.VMEM((2, rx, ry, depth), f32),
            pltpu.VMEM((rx, ry, depth), f32),
            pltpu.VMEM((2, STEPS, rx, ry, depth), f32),
            pltpu.VMEM((2, rx, ry, depth), f32),
            pltpu.VMEM((rx, ry, depth), f32),
            pltpu.VMEM((rx, ry, depth), f32),
            pltpu.VMEM((n_shot - 1, rx // n_shot, ry, depth), f32),
            pltpu.VMEM((STEPS, 2, 2, rx, W, depth), f32),
            pltpu.VMEM((STEPS, 2, 2, rx, W, depth), f32),
            dma((7,)),
            dma((STEPS, 2, 2)),
            dma((STEPS, 2, 2)),
            dma((STEPS, 2, 2)),
            dma((STEPS, 2, 2)),
            dma((n_shot - 1,)),
            dma((n_shot - 1,)),
            dma((n_shot - 1,)),
            dma((n_shot - 1,)),
            dma((3,)),
        ],
        compiler_params=pltpu.CompilerParams(
            collective_id=0, has_side_effects=True, vmem_limit_bytes=VMEM_LIMIT
        ),
        name="window",
    )(
        forward_now[0], forward_later[0], adjoint_now[0], adjoint_later[0], courant, add_p, add_q,
    )
    return out_p[None], out_q[None], out_g


def solution(mesh):
    field = P("shot", "gx", "gy", None)
    listed = P("shot", None, None)
    sizes = (mesh.shape["shot"], mesh.shape["gx"], mesh.shape["gy"])
    return jax.shard_map(
        functools.partial(shards, sizes),
        mesh=mesh,
        in_specs=(field, field, field, field, P("gx", "gy", None), listed, listed, listed, listed),
        out_specs=(field, field, P("gx", "gy", None)),
        check_vma=False,
    )
```

time: 265 us -> 88.8 us (0.34)
  the two profiles are of different devices: /device:TPU:8 before, /device:TPU:184 now
where the time goes in v1:
time: 88.8 us; the launch traced here: 88.2 us
  Pallas kernels  75.3 us (85%)
  local copies, waits for them, and re-layouts  8.81 us (10%)
  other arithmetic  3.44 us (4%)
    pallas_call x1, Pallas kernels, shards(): pl.pallas_call(functools.partial(wave_kernel, sizes), out_shape=(block, b...  72.3 us
    unnamed x15, local copies, waits for them, and re-layouts  8.72 us
    pallas_call x1, Pallas kernels, shards(): pl.pallas_call(functools.partial(scatter_kernel, rx, ry, chunks), out_sha...  2.95 us

profile of v1, /device:TPU:184, one launch (start us, length us, event | category | flops | bytes accessed | tf_op | source)
XLA Modules:
  0.0 88.2 jit_solution(12320194632252358996)
XLA Ops:
  0.6 0.1 pad_add_fusion
  0.7 0.1 pad.8.clone
  0.8 0.8 fusion.3
  1.5 0.7 bitcast_reduce-precision_fusion.1
  2.2 0.1 maximum_maximum_fusion.1
  2.3 0.9 fusion.1
  3.2 0.8 bitcast_reduce-precision_fusion
  4.1 0.1 maximum_maximum_fusion.feats_ref
  4.2 3.0 %scatter.1 = (f32[3,32,32,128]{3,2,1,0:T(8,128)S(1)}, f32[3,32,32,128]{3,2,1,0:T(8,128)S(1)}) custom-call(f32[16,4096]{1,0:T(8,128)S(1)} %maximum_maximum_fusion.feats_ref, f32[32,128]{1,0:T(8,128)S(1)} %bitcast.41, f32[16,128]{1,0:T(8,128)S(1)} %concatenate.11.sfeats_ref), custom_call_target="tpu_custom_call" | custom-call | tf_op jit(solution)/shard_map/scatter/pallas_call | solution.py:359
  7.1 0.0 copy-start
  7.1 1.1 %copy-done = f32[3,32,32,128]{3,2,1,0:T(8,128)} copy-done((f32[3,32,32,128]{3,2,1,0:T(8,128)}, f32[3,32,32,128]{3,2,1,0:T(8,128)S(1)}, u32[]{:S(2)}) %copy-start) | copy-done | bytes 1572888
  8.3 0.0 copy-start.1
  8.3 1.0 %copy-done.1 = f32[1,32,32,128]{3,2,1,0:T(8,128)S(1)} copy-done((f32[1,32,32,128]{3,2,1,0:T(8,128)S(1)}, f32[1,32,32,128]{3,2,1,0:T(8,128)}, u32[]{:S(2)}) %copy-start.1) | copy-done | bytes 524312
  9.3 0.0 copy-start.2
  9.3 1.0 %copy-done.2 = f32[1,32,32,128]{3,2,1,0:T(8,128)S(1)} copy-done((f32[1,32,32,128]{3,2,1,0:T(8,128)S(1)}, f32[1,32,32,128]{3,2,1,0:T(8,128)}, u32[]{:S(2)}) %copy-start.2) | copy-done | bytes 524312
  10.4 0.0 copy-start.3
  10.4 1.0 %copy-done.3 = f32[1,32,32,128]{3,2,1,0:T(8,128)S(1)} copy-done((f32[1,32,32,128]{3,2,1,0:T(8,128)S(1)}, f32[1,32,32,128]{3,2,1,0:T(8,128)}, u32[]{:S(2)}) %copy-start.3) | copy-done | bytes 524312
  11.4 0.0 copy-start.4
  11.4 1.0 %copy-done.4 = f32[1,32,32,128]{3,2,1,0:T(8,128)S(1)} copy-done((f32[1,32,32,128]{3,2,1,0:T(8,128)S(1)}, f32[1,32,32,128]{3,2,1,0:T(8,128)}, u32[]{:S(2)}) %copy-start.4) | copy-done | bytes 524312
  12.5 0.0 copy-start.5
  12.5 1.0 %copy-done.5 = f32[32,32,128]{2,1,0:T(8,128)S(1)} copy-done((f32[32,32,128]{2,1,0:T(8,128)S(1)}, f32[32,32,128]{2,1,0:T(8,128)}, u32[]{:S(2)}) %copy-start.5) | copy-done | bytes 524312
  13.5 72.3 %window.1 = (f32[32,32,128]{2,1,0:T(8,128)S(1)}, f32[32,32,128]{2,1,0:T(8,128)S(1)}, f32[32,32,128]{2,1,0:T(8,128)S(1)}) custom-call(f32[32,32,128]{2,1,0:T(8,128)S(1)} %bitcast.37, f32[32,32,128]{2,1,0:T(8,128)S(1)} %bitcast.38, f32[32,32,128]{2,1,0:T(8,128)S(1)} %bitcast.39, f32[32,32,128]{2,1,0:T(8,128)S(1)} %bitcast.40, f32[32,32,128]{2,1,0:T(8,128)S(1)} %copy-done.5, ...), custom_call_target="tpu_custom_call" | custom-call | tf_op jit(solution)/shard_map/window/pallas_call | solution.py:370
  85.8 0.8 copy.29
  86.6 0.8 copy.30
  87.4 0.8 copy.31
  (3 shorter events, 0.1 us)
Async XLA Ops:
  7.1 1.1 %copy-start = (f32[3,32,32,128]{3,2,1,0:T(8,128)}, f32[3,32,32,128]{3,2,1,0:T(8,128)S(1)}, u32[]{:S(2)}) copy-start(f32[3,32,32,128]{3,2,1,0:T(8,128)S(1)} %get-tuple-element.9.add_q) | copy-start | bytes 4718596
  8.3 1.0 %copy-start.1 = (f32[1,32,32,128]{3,2,1,0:T(8,128)S(1)}, f32[1,32,32,128]{3,2,1,0:T(8,128)}, u32[]{:S(2)}) copy-start(f32[1,32,32,128]{3,2,1,0:T(8,128)} %param.9) | copy-start | bytes 1572868
  9.3 1.0 %copy-start.2 = (f32[1,32,32,128]{3,2,1,0:T(8,128)S(1)}, f32[1,32,32,128]{3,2,1,0:T(8,128)}, u32[]{:S(2)}) copy-start(f32[1,32,32,128]{3,2,1,0:T(8,128)} %param.10) | copy-start | bytes 1572868
  10.4 1.0 %copy-start.3 = (f32[1,32,32,128]{3,2,1,0:T(8,128)S(1)}, f32[1,32,32,128]{3,2,1,0:T(8,128)}, u32[]{:S(2)}) copy-start(f32[1,32,32,128]{3,2,1,0:T(8,128)} %param.11) | copy-start | bytes 1572868
  11.4 1.0 %copy-start.4 = (f32[1,32,32,128]{3,2,1,0:T(8,128)S(1)}, f32[1,32,32,128]{3,2,1,0:T(8,128)}, u32[]{:S(2)}) copy-start(f32[1,32,32,128]{3,2,1,0:T(8,128)} %param.12) | copy-start | bytes 1572868
  12.5 1.0 %copy-start.5 = (f32[32,32,128]{2,1,0:T(8,128)S(1)}, f32[32,32,128]{2,1,0:T(8,128)}, u32[]{:S(2)}) copy-start(f32[32,32,128]{2,1,0:T(8,128)} %courant.1) | copy-start | bytes 1572868

commit v2 on v1

--- a/solution.py
+++ b/solution.py
@@ -15,43 +15,50 @@
 COEFFS = (-205.0 / 72.0, 8.0 / 5.0, -1.0 / 5.0, 8.0 / 315.0, -1.0 / 560.0)
 GRAD_SCALE = 0.1
 MESH = pl.DeviceIdType.MESH
-VMEM_LIMIT = 48 * 1024 * 1024
-
-
-def scatter_kernel(rows_x, rows_y, chunks, feats_ref, mask_ref, sfeats_ref, out_p, out_q, rank_ref):
+WINDOW_LIMIT = 64_000_000
+RING = 4
+
+
+def scatter_kernel(
+    rows_x, rows_y, chunks, scells, swave, cells_ref, values_ref, out_p, out_q, rank_ref, feats_ref
+):
     cells = rows_x * rows_y
     f32, bf16 = jnp.float32, jnp.bfloat16
     nt = (((1,), (1,)), ((), ()))
-
-    def spread(by_row, by_col, out, add):
-        slots = by_row.shape[1]
-        place = by_row[0:1, :] * float(rows_y) + by_row[1:2, :]
-        ids = lax.broadcasted_iota(jnp.int32, (cells, slots), 0).astype(f32)
-        left = (ids == place).astype(f32).astype(bf16)
-        lane = lax.broadcasted_iota(jnp.int32, (slots, LANES), 1).astype(f32)
-        hit = lane == by_col[:, 2:3]
-        for step in range(STEPS):
-            high = jnp.where(hit, by_col[:, 3 + step : 4 + step], 0.0)
-            low = jnp.where(hit, by_col[:, 6 + step : 7 + step], 0.0)
-            right = jnp.concatenate([high, low], axis=1).astype(bf16)
-            both = jnp.dot(left, right, preferred_element_type=f32)
-            total = (both[:, :LANES] + both[:, LANES:]).reshape(rows_x, rows_y, LANES)
-            if add:
-                out[step] = out[step] + total
-            else:
-                out[step] = total
-
-    sfeats = sfeats_ref[...]
-    inside = (
-        (sfeats[0:1] >= 0.0)
-        & (sfeats[0:1] < float(rows_x))
-        & (sfeats[1:2] >= 0.0)
-        & (sfeats[1:2] < float(rows_y))
-    )
-    sfeats = jnp.where(inside, sfeats, 0.0)
-    spread(sfeats, sfeats.T, out_p, False)
-
-    mask = mask_ref[...]
+    base_x = lax.axis_index("gx") * rows_x
+    base_y = lax.axis_index("gy") * rows_y
+    out_p[...] = jnp.zeros_like(out_p)
+    out_q[...] = jnp.zeros_like(out_q)
+
+    depth_ids = lax.broadcasted_iota(jnp.int32, (1, LANES), 1)
+
+    def one_source(i, carry):
+        x = scells[i, 0] - base_x
+        y = scells[i, 1] - base_y
+
+        @pl.when((x >= 0) & (x < rows_x) & (y >= 0) & (y < rows_y))
+        def _():
+            for step in range(STEPS):
+                line = out_p[step, x, pl.ds(y, 1), :]
+                out_p[step, x, pl.ds(y, 1), :] = line + jnp.where(depth_ids == scells[i, 2], swave[step, i], 0.0)
+
+        return carry
+
+    lax.fori_loop(0, scells.shape[0], one_source, 0)
+
+    x = (cells_ref[0:chunks, :] - base_x).astype(f32)
+    y = (cells_ref[chunks : 2 * chunks, :] - base_y).astype(f32)
+    inside = (x >= 0.0) & (x < float(rows_x)) & (y >= 0.0) & (y < float(rows_y))
+    mask = jnp.where(inside, 1.0, 0.0)
+    high = values_ref[...].astype(bf16).astype(f32)
+    low = values_ref[...] - high
+    parts = [x, y, cells_ref[2 * chunks : 3 * chunks, :].astype(f32)]
+    parts += [high[s * chunks : (s + 1) * chunks] for s in range(STEPS)]
+    parts += [low[s * chunks : (s + 1) * chunks] for s in range(STEPS)]
+    feats_ref[...] = jnp.zeros_like(feats_ref)
+    for i, values in enumerate(parts):
+        for chunk in range(chunks):
+            feats_ref[16 * chunk + i : 16 * chunk + i + 1, :] = values[chunk : chunk + 1, :]
     ones = mask.astype(bf16)
     row = lax.broadcasted_iota(jnp.int32, (LANES, LANES), 0)
     col = lax.broadcasted_iota(jnp.int32, (LANES, LANES), 1)
@@ -62,9 +69,8 @@
     ccol = lax.broadcasted_iota(jnp.int32, (chunks, chunks), 1)
     before = (ccol < crow).astype(f32).astype(bf16)
     offsets = jnp.dot(before, totals, preferred_element_type=f32)
-    rank_ref[...] = jnp.where(mask > 0.5, offsets + inclusive - 1.0, -1.0)
+    rank_ref[...] = jnp.where(inside, offsets + inclusive - 1.0, -1.0)
     count = jnp.sum(mask).astype(jnp.int32)
-    out_q[...] = jnp.zeros_like(out_q)
 
     def one_round(turn, carry):
         slot = lax.broadcasted_iota(jnp.int32, (SLOTS, LANES), 0).astype(f32)
@@ -74,32 +80,43 @@
         for chunk in range(chunks):
             rank = rank_ref[chunk : chunk + 1, :] - base
             pick = (slot == rank).astype(f32).astype(bf16)
-            part = feats_ref[:, chunk * LANES : (chunk + 1) * LANES].astype(bf16)
+            part = feats_ref[16 * chunk : 16 * chunk + 16, :].astype(bf16)
             by_row = by_row + lax.dot_general(part, pick, nt, preferred_element_type=f32)
             by_col = by_col + lax.dot_general(pick, part, nt, preferred_element_type=f32)
-        spread(by_row, by_col, out_q, True)
+        place = by_row[0:1, :] * float(rows_y) + by_row[1:2, :]
+        ids = lax.broadcasted_iota(jnp.int32, (cells, SLOTS), 0).astype(f32)
+        left = (ids == place).astype(f32).astype(bf16)
+        lane = lax.broadcasted_iota(jnp.int32, (SLOTS, LANES), 1).astype(f32)
+        hit = lane == by_col[:, 2:3]
+        for step in range(STEPS):
+            upper_part = jnp.where(hit, by_col[:, 3 + step : 4 + step], 0.0)
+            lower_part = jnp.where(hit, by_col[:, 6 + step : 7 + step], 0.0)
+            right = jnp.concatenate([upper_part, lower_part], axis=1).astype(bf16)
+            both = jnp.dot(left, right, preferred_element_type=f32)
+            total = (both[:, :LANES] + both[:, LANES:]).reshape(rows_x, rows_y, LANES)
+            out_q[step] = out_q[step] + total
         return carry
 
     lax.fori_loop(0, (count + SLOTS - 1) // SLOTS, one_round, 0)
 
 
-def features(cells, values, start_x, start_y):
-    count = cells.shape[0]
-    high = lax.reduce_precision(values, 8, 7)
-    local = cells.T - jnp.stack([start_x, start_y, jnp.int32(0)])[:, None]
-    rows = [local.astype(jnp.float32), high, values - high, jnp.zeros((7, count), jnp.float32)]
-    padded = -(-count // LANES) * LANES
-    if padded == count:
-        return jnp.concatenate(rows, 0)
-    rows = jnp.concatenate(rows, 0)
-    tail = jnp.full((16, padded - count), -1.0, jnp.float32)
-    return jnp.concatenate([rows, tail], 1)
+def finish_kernel(a, b, c, out_a, out_b, out_c, buf, sems_in, sems_out):
+    pairs = ((a, out_a), (b, out_b), (c, out_c))
+    ins = [pltpu.make_async_copy(src, buf.at[i], sems_in.at[i]) for i, (src, _) in enumerate(pairs)]
+    outs = [pltpu.make_async_copy(buf.at[i], dst, sems_out.at[i]) for i, (_, dst) in enumerate(pairs)]
+    for copy in ins:
+        copy.start()
+    for copy_in, copy_out in zip(ins, outs):
+        copy_in.wait()
+        copy_out.start()
+    for copy in outs:
+        copy.wait()
 
 
 def wave_kernel(
     sizes, p0, p2, q0, q2, courant, add_p, add_q, out_p, out_q, out_g,
-    ext, last, cour, adds, final, gacc, gout, rbuf, ysend, yrecv,
-    load_sem, xs, xr, ys, yr, gs, gr, hs, hr, store_sem,
+    ext, last, cour, adds, final, gacc, gout, rbuf_a, rbuf_b, ysend, yrecv, relay,
+    load_sem, xs, xr, ys, yr, gs, gr, hs, hr, ls, lr, store_sem,
 ):
     n_shot, n_gx, n_gy, rx, ry = sizes
     me_s = lax.axis_index("shot")
@@ -108,7 +125,9 @@
     fields = (p0, q0)
     mid_x = pl.ds(W, rx)
     mid_y = pl.ds(PADY, ry)
-    part = rx // n_shot
+    ring = lax.rem(me_x, RING)
+    group = me_x // RING
+    groups = n_gx // RING
 
     loads = []
 
@@ -165,6 +184,42 @@
     expected = n_shot - 1
     for k in range(4):
         expected = expected + has[k].astype(jnp.int32)
+
+    last_of = ring == RING - 1
+    first_of = ring == 0
+    crosses = ((last_of & has[0]), (first_of & has[1]))
+    relays = ([r for r in range(1, RING)], [r for r in range(RING - 1)])
+    straight = (0, RING - 1)
+    home = group * RING
+
+    def relay_id(side, r):
+        target = home + RING + r if side == 0 else home - RING + r
+        return {"gx": jnp.clip(target, 0, n_gx - 1)}
+
+    def is_relay(side, r):
+        there = (group > 0) if side == 0 else (group < groups - 1)
+        return (ring == r) & there
+
+    def relay_source(side):
+        return {"gx": jnp.clip(home - 1 if side == 0 else home + RING, 0, n_gx - 1)}
+
+    def relay_target(side):
+        return {"gx": home if side == 0 else home + RING - 1}
+
+    def greet(condition, who):
+        @pl.when(condition)
+        def _():
+            pl.semaphore_signal(barrier, inc=1, device_id=who, device_id_type=MESH)
+
+        return condition.astype(jnp.int32)
+
+    for side in range(2):
+        for r in relays[side]:
+            expected = expected + greet(crosses[side], relay_id(side, r))
+            expected = expected + greet(is_relay(side, r), relay_source(side))
+            expected = expected + greet(is_relay(side, r), relay_target(side))
+            takes = crosses[1 - side]
+            expected = expected + greet(takes, {"gx": home + r})
     pl.semaphore_wait(barrier, expected)
 
     def x_copy(step, f, side):
@@ -175,7 +230,7 @@
             src = ext.at[step, f, pl.ds(W + first, W), mid_y]
         dst = ext.at[step, f, pl.ds(0 if side == 0 else W + rx, W), mid_y]
         return pltpu.make_async_remote_copy(
-            src_ref=src, dst_ref=dst, send_sem=xs.at[step, f, side], recv_sem=xr.at[step, f, side],
+            src_ref=src, dst_ref=dst, send_sem=xs.at[step, f, side, 0], recv_sem=xr.at[step, f, side, 0],
             device_id=ids[side], device_id_type=MESH,
         )
 
@@ -186,10 +241,54 @@
             device_id=ids[2 + side], device_id_type=MESH,
         )
 
+    def piece_copy(step, f, side, piece):
+        first = (rx - W) if side == 0 else 0
+        if step == 0:
+            src = fields[f].at[pl.ds(first + piece, 1)]
+        else:
+            src = ext.at[step, f, pl.ds(W + first + piece, 1), mid_y]
+        if piece == straight[side]:
+            dst = ext.at[step, f, pl.ds((0 if side == 0 else W + rx) + piece, 1), mid_y]
+            sem, who = xr.at[step, f, side, piece], ids[side]
+        else:
+            dst = relay.at[step, f, side]
+            sem, who = lr.at[step, f, side], relay_id(side, piece)
+        return pltpu.make_async_remote_copy(
+            src_ref=src, dst_ref=dst, send_sem=xs.at[step, f, side, piece], recv_sem=sem,
+            device_id=who, device_id_type=MESH,
+        )
+
+    def relay_copy(step, f, side, piece):
+        return pltpu.make_async_remote_copy(
+            src_ref=relay.at[step, f, side],
+            dst_ref=ext.at[step, f, pl.ds((0 if side == 0 else W + rx) + piece, 1), mid_y],
+            send_sem=ls.at[step, f, side], recv_sem=xr.at[step, f, side, piece],
+            device_id=relay_target(side), device_id_type=MESH,
+        )
+
+    def pass_on(step, f):
+        for side in range(2):
+            for r in relays[side]:
+
+                @pl.when(is_relay(side, r))
+                def _():
+                    copy = relay_copy(step, f, side, r)
+                    pltpu.make_async_remote_copy(
+                        src_ref=relay.at[step, f, side], dst_ref=relay.at[step, f, side],
+                        send_sem=ls.at[step, f, side], recv_sem=lr.at[step, f, side],
+                        device_id=relay_target(side), device_id_type=MESH,
+                    ).wait_recv()
+                    copy.start()
+
     def start_x(step, f):
         for side in range(2):
 
-            @pl.when(has[side])
+            @pl.when(crosses[side])
+            def _():
+                for piece in range(W):
+                    piece_copy(step, f, side, piece).start()
+
+            @pl.when(has[side] & ~crosses[side])
             def _():
                 x_copy(step, f, side).start()
 
@@ -205,7 +304,12 @@
     def wait_x(step, f):
         for side in range(2):
 
-            @pl.when(has[1 - side])
+            @pl.when(crosses[1 - side])
+            def _():
+                for piece in range(W):
+                    relay_copy(step, f, side, piece).wait_recv()
+
+            @pl.when(has[1 - side] & ~crosses[1 - side])
             def _():
                 x_copy(step, f, side).wait_recv()
 
@@ -269,54 +373,87 @@
     for copy in loads[2:]:
         copy.wait()
     stores = []
-    reduce_sends = []
+    sends = []
+    part_a = (rx - 2 * W) // n_shot
+    part_b = 2 * W // n_shot
+
+    def start_a(s):
+        return W + s * part_a
+
+    def start_b(s):
+        return s * part_b + (s // (n_shot // 2)) * (rx - 2 * W)
+
+    kinds = ((part_a, start_a, rbuf_a), (part_b, start_b, rbuf_b))
+
+    def reduce_start(kind):
+        size, start, buf = kinds[kind]
+        copies = []
+        for d, peer in enumerate(peers):
+            copy = pltpu.make_async_remote_copy(
+                src_ref=gacc.at[pl.ds(start(peer), size)], dst_ref=buf.at[d],
+                send_sem=gs.at[kind, d], recv_sem=gr.at[kind, d],
+                device_id={"shot": peer}, device_id_type=MESH,
+            )
+            copy.start()
+            copies.append(copy)
+        sends.extend(copies)
+        return copies
+
+    def reduce_end(kind, copies):
+        size, start, buf = kinds[kind]
+        mine = pl.ds(start(me_s), size)
+        for copy in copies:
+            copy.wait_recv()
+        total = gacc[mine]
+        for d in range(n_shot - 1):
+            total = total + buf[d]
+        gout[mine] = total * ((2.0 * GRAD_SCALE) * cour[mine])
+        for d, peer in enumerate(peers):
+            copy = pltpu.make_async_remote_copy(
+                src_ref=gout.at[mine], dst_ref=gout.at[mine],
+                send_sem=hs.at[kind, d], recv_sem=hr.at[kind, d],
+                device_id={"shot": peer}, device_id_type=MESH,
+            )
+            copy.start()
+            sends.append(copy)
+
+    def gather_wait(kind):
+        size, start, buf = kinds[kind]
+        for d in range(n_shot - 1):
+            other = lax.rem(me_s + n_shot - 1 - d, n_shot)
+            theirs = gout.at[pl.ds(start(other), size)]
+            pltpu.make_async_remote_copy(
+                src_ref=theirs, dst_ref=theirs, send_sem=hs.at[kind, d], recv_sem=hr.at[kind, d],
+                device_id={"shot": other}, device_id_type=MESH,
+            ).wait_recv()
+
+    end = STEPS - 1
     for step in range(STEPS):
         for f in range(2):
             wait_y(step, f)
             planes(step, f, W, rx - W)
+            if step == end and f == 0:
+                inner = reduce_start(0)
+        for f in range(2):
+            pass_on(step, f)
+        if step == end:
+            reduce_end(0, inner)
         for f in range(2):
             wait_x(step, f)
             planes(step, f, 0, W)
             planes(step, f, rx - W, rx)
-            if step < STEPS - 1:
+            if step < end:
                 start_x(step + 1, f)
                 start_y(step + 1, f)
             else:
+                if f == 0:
+                    outer = reduce_start(1)
                 copy = pltpu.make_async_copy(final.at[f], (out_p, out_q)[f], store_sem.at[f])
                 copy.start()
                 stores.append(copy)
-            if step == STEPS - 1 and f == 0:
-                for d, peer in enumerate(peers):
-                    copy = pltpu.make_async_remote_copy(
-                        src_ref=gacc.at[pl.ds(peer * part, part)], dst_ref=rbuf.at[d],
-                        send_sem=gs.at[d], recv_sem=gr.at[d],
-                        device_id={"shot": peer}, device_id_type=MESH,
-                    )
-                    copy.start()
-                    reduce_sends.append(copy)
-
-    for copy in reduce_sends:
-        copy.wait_recv()
-    mine = pl.ds(me_s * part, part)
-    total = gacc[mine]
-    for d in range(n_shot - 1):
-        total = total + rbuf[d]
-    gout[mine] = total * ((2.0 * GRAD_SCALE) * cour[mine])
-    gathers = []
-    for d, peer in enumerate(peers):
-        copy = pltpu.make_async_remote_copy(
-            src_ref=gout.at[mine], dst_ref=gout.at[mine], send_sem=hs.at[d], recv_sem=hr.at[d],
-            device_id={"shot": peer}, device_id_type=MESH,
-        )
-        copy.start()
-        gathers.append(copy)
-    for d, copy in enumerate(gathers):
-        other = lax.rem(me_s + n_shot - 1 - d, n_shot)
-        theirs = gout.at[pl.ds(other * part, part)]
-        pltpu.make_async_remote_copy(
-            src_ref=theirs, dst_ref=theirs, send_sem=hs.at[d], recv_sem=hr.at[d],
-            device_id={"shot": other}, device_id_type=MESH,
-        ).wait_recv()
+    reduce_end(1, outer)
+    gather_wait(0)
+    gather_wait(1)
     copy = pltpu.make_async_copy(gout, out_g, store_sem.at[2])
     copy.start()
     stores.append(copy)
@@ -324,15 +461,26 @@
         for f in range(2):
             for side in range(2):
 
-                @pl.when(has[side])
+                @pl.when(crosses[side])
+                def _():
+                    for piece in range(W):
+                        piece_copy(step, f, side, piece).wait_send()
+
+                @pl.when(has[side] & ~crosses[side])
                 def _():
                     x_copy(step, f, side).wait_send()
+
+                for r in relays[side]:
+
+                    @pl.when(is_relay(side, r))
+                    def _():
+                        relay_copy(step, f, side, r).wait_send()
 
                 @pl.when(has[2 + side])
                 def _():
                     y_copy(step, f, side).wait_send()
 
-    for copy in reduce_sends + gathers:
+    for copy in sends:
         copy.wait_send()
     for copy in stores:
         copy.wait()
@@ -345,13 +493,10 @@
     rx, ry, depth = courant.shape
     n_shot, n_gx, n_gy = mesh_sizes
     f32 = jnp.float32
-    start_x = (lax.axis_index("gx") * rx).astype(jnp.int32)
-    start_y = (lax.axis_index("gy") * ry).astype(jnp.int32)
-    feats = features(receiver_cells[0], residual[0], start_x, start_y)
-    sfeats = features(source_cells[0], source_wave[0], start_x, start_y)
-    mask = (feats[0] >= 0) & (feats[0] < rx) & (feats[1] >= 0) & (feats[1] < ry)
-    chunks = feats.shape[1] // LANES
-    mask = mask.astype(f32).reshape(chunks, LANES)
+    chunks = receiver_cells.shape[1] // LANES
+    cells = jnp.transpose(receiver_cells, (2, 0, 1)).reshape(3 * chunks, LANES)
+    values = residual[0].reshape(STEPS * chunks, LANES)
+    scalars = pl.BlockSpec(memory_space=pltpu.SMEM)
     whole = pl.BlockSpec(memory_space=pltpu.VMEM)
     anywhere = pl.BlockSpec(memory_space=pl.ANY)
     block = jax.ShapeDtypeStruct((rx, ry, depth), f32)
@@ -359,12 +504,12 @@
     add_p, add_q = pl.pallas_call(
         functools.partial(scatter_kernel, rx, ry, chunks),
         out_shape=(added, added),
-        in_specs=[whole] * 3,
+        in_specs=[scalars] * 2 + [whole] * 2,
         out_specs=(whole, whole),
-        scratch_shapes=[pltpu.VMEM((chunks, LANES), f32)],
-        compiler_params=pltpu.CompilerParams(vmem_limit_bytes=VMEM_LIMIT),
+        scratch_shapes=[pltpu.VMEM((chunks, LANES), f32), pltpu.VMEM((16 * chunks, LANES), f32)],
+        compiler_params=pltpu.CompilerParams(vmem_limit_bytes=WINDOW_LIMIT),
         name="scatter",
-    )(feats, mask, sfeats)
+    )(source_cells[0], source_wave[0], cells, values)
     sizes = (n_shot, n_gx, n_gy, rx, ry)
     dma = pltpu.SemaphoreType.DMA
     out_p, out_q, out_g = pl.pallas_call(
@@ -380,27 +525,40 @@
             pltpu.VMEM((2, rx, ry, depth), f32),
             pltpu.VMEM((rx, ry, depth), f32),
             pltpu.VMEM((rx, ry, depth), f32),
-            pltpu.VMEM((n_shot - 1, rx // n_shot, ry, depth), f32),
+            pltpu.VMEM((n_shot - 1, (rx - 2 * W) // n_shot, ry, depth), f32),
+            pltpu.VMEM((n_shot - 1, 2 * W // n_shot, ry, depth), f32),
             pltpu.VMEM((STEPS, 2, 2, rx, W, depth), f32),
             pltpu.VMEM((STEPS, 2, 2, rx, W, depth), f32),
+            pltpu.VMEM((STEPS, 2, 2, 1, ry, depth), f32),
             dma((7,)),
+            dma((STEPS, 2, 2, W)),
+            dma((STEPS, 2, 2, W)),
             dma((STEPS, 2, 2)),
             dma((STEPS, 2, 2)),
+            dma((2, n_shot - 1)),
+            dma((2, n_shot - 1)),
+            dma((2, n_shot - 1)),
+            dma((2, n_shot - 1)),
             dma((STEPS, 2, 2)),
             dma((STEPS, 2, 2)),
-            dma((n_shot - 1,)),
-            dma((n_shot - 1,)),
-            dma((n_shot - 1,)),
-            dma((n_shot - 1,)),
             dma((3,)),
         ],
         compiler_params=pltpu.CompilerParams(
-            collective_id=0, has_side_effects=True, vmem_limit_bytes=VMEM_LIMIT
+            collective_id=0, has_side_effects=True, vmem_limit_bytes=WINDOW_LIMIT
         ),
         name="window",
     )(
         forward_now[0], forward_later[0], adjoint_now[0], adjoint_later[0], courant, add_p, add_q,
     )
+    out_p, out_q, out_g = pl.pallas_call(
+        finish_kernel,
+        out_shape=(block, block, block),
+        in_specs=[anywhere] * 3,
+        out_specs=(anywhere,) * 3,
+        scratch_shapes=[pltpu.VMEM((3, rx, ry, depth), f32), dma((3,)), dma((3,))],
+        compiler_params=pltpu.CompilerParams(vmem_limit_bytes=WINDOW_LIMIT),
+        name="finish",
+    )(out_p, out_q, out_g)
     return out_p[None], out_q[None], out_g
 
 

time: 88.8 us -> 93.8 us (1.056)
  the two profiles are of different devices: /device:TPU:184 before, /device:TPU:152 now
where the time goes in v2:
time: 93.8 us; the launch traced here: 93.5 us
  Pallas kernels  90.3 us (96%)
  local copies, waits for them, and re-layouts  2.61 us (3%)
    pallas_call x1, Pallas kernels, shards(): pl.pallas_call(functools.partial(wave_kernel, sizes), out_shape=(block, b...  82.8 us
    pallas_call x1, Pallas kernels, shards(): pl.pallas_call(functools.partial(scatter_kernel, rx, ry, chunks), out_sha...  5.26 us
    pallas_call x1, Pallas kernels, shards(): pl.pallas_call(finish_kernel, out_shape=(block, block, block), in_specs=[...  2.23 us

profile of v2, /device:TPU:152, one launch (start us, length us, event | category | flops | bytes accessed | tf_op | source)
XLA Modules:
  0.0 93.5 jit_solution(10602692883306868867)
XLA Ops:
  0.6 1.3 %copy.16 = f32[1,3,16]{2,1,0:T(4,128)} copy(f32[1,3,16]{2,0,1:T(1,128)} %param.15) | data formatting | bytes 384
  1.9 1.4 %copy.13 = s32[1,16,3]{2,1,0:T(8,128)} copy(s32[1,16,3]{1,0,2:T(1,128)} %param.14) | data formatting | bytes 384 | tf_op jit(solution)/shard_map/squeeze | solution.py:512
  3.2 5.3 %scatter.1 = (f32[3,32,32,128]{3,2,1,0:T(8,128)}, f32[3,32,32,128]{3,2,1,0:T(8,128)}) custom-call(s32[16,3]{1,0:T(8,128)} %bitcast.20, f32[3,16]{1,0:T(4,128)} %bitcast.21, s32[96,128]{1,0:T(8,128)} %bitcast.18, f32[96,128]{1,0:T(8,128)} %bitcast.19), custom_call_target="tpu_custom_call" | custom-call | tf_op jit(solution)/shard_map/scatter/pallas_call | solution.py:504
  8.5 82.8 %window.1 = (f32[32,32,128]{2,1,0:T(8,128)}, f32[32,32,128]{2,1,0:T(8,128)}, f32[32,32,128]{2,1,0:T(8,128)}) custom-call(f32[32,32,128]{2,1,0:T(8,128)} %bitcast.14, f32[32,32,128]{2,1,0:T(8,128)} %bitcast.15, f32[32,32,128]{2,1,0:T(8,128)} %bitcast.16, f32[32,32,128]{2,1,0:T(8,128)} %bitcast.17, f32[32,32,128]{2,1,0:T(8,128)} %courant.1, ...), custom_call_target="tpu_custom_call" | custom-call | tf_op jit(solution)/shard_map/window/pallas_call | solution.py:515
  91.3 2.2 %finish.1 = (f32[32,32,128]{2,1,0:T(8,128)}, f32[32,32,128]{2,1,0:T(8,128)}, f32[32,32,128]{2,1,0:T(8,128)}) custom-call(f32[32,32,128]{2,1,0:T(8,128)} %get-tuple-element.13.a, f32[32,32,128]{2,1,0:T(8,128)} %get-tuple-element.14.b, f32[32,32,128]{2,1,0:T(8,128)} %get-tuple-element.15.c), custom_call_target="tpu_custom_call" | custom-call | tf_op jit(solution)/shard_map/finish/pallas_call | solution.py:553

commit v3 on v2

--- a/solution.py
+++ b/solution.py
@@ -16,7 +16,7 @@
 GRAD_SCALE = 0.1
 MESH = pl.DeviceIdType.MESH
 WINDOW_LIMIT = 64_000_000
-RING = 4
+UNROLL = 4
 
 
 def scatter_kernel(
@@ -115,8 +115,8 @@
 
 def wave_kernel(
     sizes, p0, p2, q0, q2, courant, add_p, add_q, out_p, out_q, out_g,
-    ext, last, cour, adds, final, gacc, gout, rbuf_a, rbuf_b, ysend, yrecv, relay,
-    load_sem, xs, xr, ys, yr, gs, gr, hs, hr, ls, lr, store_sem,
+    ext, last, cour, adds, final, gacc, gout, rbuf_a, rbuf_b, ysend, yrecv,
+    load_sem, xs, xr, ys, yr, gs, gr, hs, hr, store_sem,
 ):
     n_shot, n_gx, n_gy, rx, ry = sizes
     me_s = lax.axis_index("shot")
@@ -125,10 +125,6 @@
     fields = (p0, q0)
     mid_x = pl.ds(W, rx)
     mid_y = pl.ds(PADY, ry)
-    ring = lax.rem(me_x, RING)
-    group = me_x // RING
-    groups = n_gx // RING
-
     loads = []
 
     def load(src, dst):
@@ -141,8 +137,9 @@
     load(courant, cour)
     load(p2, last.at[0])
     load(q2, last.at[1])
-    load(add_p, adds.at[0])
-    load(add_q, adds.at[1])
+    for step in range(STEPS):
+        load(add_p.at[step], adds.at[0, step])
+        load(add_q.at[step], adds.at[1, step])
 
     for step in range(STEPS):
         for f in range(2):
@@ -185,41 +182,6 @@
     for k in range(4):
         expected = expected + has[k].astype(jnp.int32)
 
-    last_of = ring == RING - 1
-    first_of = ring == 0
-    crosses = ((last_of & has[0]), (first_of & has[1]))
-    relays = ([r for r in range(1, RING)], [r for r in range(RING - 1)])
-    straight = (0, RING - 1)
-    home = group * RING
-
-    def relay_id(side, r):
-        target = home + RING + r if side == 0 else home - RING + r
-        return {"gx": jnp.clip(target, 0, n_gx - 1)}
-
-    def is_relay(side, r):
-        there = (group > 0) if side == 0 else (group < groups - 1)
-        return (ring == r) & there
-
-    def relay_source(side):
-        return {"gx": jnp.clip(home - 1 if side == 0 else home + RING, 0, n_gx - 1)}
-
-    def relay_target(side):
-        return {"gx": home if side == 0 else home + RING - 1}
-
-    def greet(condition, who):
-        @pl.when(condition)
-        def _():
-            pl.semaphore_signal(barrier, inc=1, device_id=who, device_id_type=MESH)
-
-        return condition.astype(jnp.int32)
-
-    for side in range(2):
-        for r in relays[side]:
-            expected = expected + greet(crosses[side], relay_id(side, r))
-            expected = expected + greet(is_relay(side, r), relay_source(side))
-            expected = expected + greet(is_relay(side, r), relay_target(side))
-            takes = crosses[1 - side]
-            expected = expected + greet(takes, {"gx": home + r})
     pl.semaphore_wait(barrier, expected)
 
     def x_copy(step, f, side):
@@ -230,7 +192,7 @@
             src = ext.at[step, f, pl.ds(W + first, W), mid_y]
         dst = ext.at[step, f, pl.ds(0 if side == 0 else W + rx, W), mid_y]
         return pltpu.make_async_remote_copy(
-            src_ref=src, dst_ref=dst, send_sem=xs.at[step, f, side, 0], recv_sem=xr.at[step, f, side, 0],
+            src_ref=src, dst_ref=dst, send_sem=xs.at[step, f, side], recv_sem=xr.at[step, f, side],
             device_id=ids[side], device_id_type=MESH,
         )
 
@@ -241,54 +203,10 @@
             device_id=ids[2 + side], device_id_type=MESH,
         )
 
-    def piece_copy(step, f, side, piece):
-        first = (rx - W) if side == 0 else 0
-        if step == 0:
-            src = fields[f].at[pl.ds(first + piece, 1)]
-        else:
-            src = ext.at[step, f, pl.ds(W + first + piece, 1), mid_y]
-        if piece == straight[side]:
-            dst = ext.at[step, f, pl.ds((0 if side == 0 else W + rx) + piece, 1), mid_y]
-            sem, who = xr.at[step, f, side, piece], ids[side]
-        else:
-            dst = relay.at[step, f, side]
-            sem, who = lr.at[step, f, side], relay_id(side, piece)
-        return pltpu.make_async_remote_copy(
-            src_ref=src, dst_ref=dst, send_sem=xs.at[step, f, side, piece], recv_sem=sem,
-            device_id=who, device_id_type=MESH,
-        )
-
-    def relay_copy(step, f, side, piece):
-        return pltpu.make_async_remote_copy(
-            src_ref=relay.at[step, f, side],
-            dst_ref=ext.at[step, f, pl.ds((0 if side == 0 else W + rx) + piece, 1), mid_y],
-            send_sem=ls.at[step, f, side], recv_sem=xr.at[step, f, side, piece],
-            device_id=relay_target(side), device_id_type=MESH,
-        )
-
-    def pass_on(step, f):
-        for side in range(2):
-            for r in relays[side]:
-
-                @pl.when(is_relay(side, r))
-                def _():
-                    copy = relay_copy(step, f, side, r)
-                    pltpu.make_async_remote_copy(
-                        src_ref=relay.at[step, f, side], dst_ref=relay.at[step, f, side],
-                        send_sem=ls.at[step, f, side], recv_sem=lr.at[step, f, side],
-                        device_id=relay_target(side), device_id_type=MESH,
-                    ).wait_recv()
-                    copy.start()
-
     def start_x(step, f):
         for side in range(2):
 
-            @pl.when(crosses[side])
-            def _():
-                for piece in range(W):
-                    piece_copy(step, f, side, piece).start()
-
-            @pl.when(has[side] & ~crosses[side])
+            @pl.when(has[side])
             def _():
                 x_copy(step, f, side).start()
 
@@ -304,12 +222,7 @@
     def wait_x(step, f):
         for side in range(2):
 
-            @pl.when(crosses[1 - side])
-            def _():
-                for piece in range(W):
-                    relay_copy(step, f, side, piece).wait_recv()
-
-            @pl.when(has[1 - side] & ~crosses[1 - side])
+            @pl.when(has[1 - side])
             def _():
                 x_copy(step, f, side).wait_recv()
 
@@ -358,11 +271,12 @@
             final[f, x] = fresh
 
     def planes(step, f, low, high):
-        def body(x, carry):
-            advance(step, f, x)
+        def body(i, carry):
+            for k in range(UNROLL):
+                advance(step, f, low + i * UNROLL + k)
             return carry
 
-        lax.fori_loop(low, high, body, 0)
+        lax.fori_loop(0, (high - low) // UNROLL, body, 0)
 
     for f in range(2):
         start_x(0, f)
@@ -370,7 +284,7 @@
     start_y(0, 0)
     loads[1].wait()
     start_y(0, 1)
-    for copy in loads[2:]:
+    for copy in loads[2:5]:
         copy.wait()
     stores = []
     sends = []
@@ -430,12 +344,11 @@
     end = STEPS - 1
     for step in range(STEPS):
         for f in range(2):
+            loads[5 + 2 * step + f].wait()
             wait_y(step, f)
             planes(step, f, W, rx - W)
             if step == end and f == 0:
                 inner = reduce_start(0)
-        for f in range(2):
-            pass_on(step, f)
         if step == end:
             reduce_end(0, inner)
         for f in range(2):
@@ -461,20 +374,9 @@
         for f in range(2):
             for side in range(2):
 
-                @pl.when(crosses[side])
-                def _():
-                    for piece in range(W):
-                        piece_copy(step, f, side, piece).wait_send()
-
-                @pl.when(has[side] & ~crosses[side])
+                @pl.when(has[side])
                 def _():
                     x_copy(step, f, side).wait_send()
-
-                for r in relays[side]:
-
-                    @pl.when(is_relay(side, r))
-                    def _():
-                        relay_copy(step, f, side, r).wait_send()
 
                 @pl.when(has[2 + side])
                 def _():
@@ -529,18 +431,15 @@
             pltpu.VMEM((n_shot - 1, 2 * W // n_shot, ry, depth), f32),
             pltpu.VMEM((STEPS, 2, 2, rx, W, depth), f32),
             pltpu.VMEM((STEPS, 2, 2, rx, W, depth), f32),
-            pltpu.VMEM((STEPS, 2, 2, 1, ry, depth), f32),
-            dma((7,)),
-            dma((STEPS, 2, 2, W)),
-            dma((STEPS, 2, 2, W)),
+            dma((5 + 2 * STEPS,)),
+            dma((STEPS, 2, 2)),
+            dma((STEPS, 2, 2)),
             dma((STEPS, 2, 2)),
             dma((STEPS, 2, 2)),
             dma((2, n_shot - 1)),
             dma((2, n_shot - 1)),
             dma((2, n_shot - 1)),
             dma((2, n_shot - 1)),
-            dma((STEPS, 2, 2)),
-            dma((STEPS, 2, 2)),
             dma((3,)),
         ],
         compiler_params=pltpu.CompilerParams(

time: 93.8 us -> 81.4 us (0.87)
  the two profiles are of different devices: /device:TPU:152 before, /device:TPU:120 now
where the time goes in v3:
time: 81.4 us; the launch traced here: 81.2 us
  Pallas kernels  77.9 us (96%)
  local copies, waits for them, and re-layouts  2.61 us (3%)
    pallas_call x1, Pallas kernels, shards(): pl.pallas_call(functools.partial(wave_kernel, sizes), out_shape=(block, b...  70.4 us
    pallas_call x1, Pallas kernels, shards(): pl.pallas_call(functools.partial(scatter_kernel, rx, ry, chunks), out_sha...  5.26 us
    pallas_call x1, Pallas kernels, shards(): pl.pallas_call(finish_kernel, out_shape=(block, block, block), in_specs=[...  2.23 us

profile of v3, /device:TPU:120, one launch (start us, length us, event | category | flops | bytes accessed | tf_op | source)
XLA Modules:
  0.0 81.2 jit_solution(1723387842828018345)
XLA Ops:
  0.6 1.3 %copy.16 = f32[1,3,16]{2,1,0:T(4,128)} copy(f32[1,3,16]{2,0,1:T(1,128)} %param.15) | data formatting | bytes 384
  1.9 1.4 %copy.13 = s32[1,16,3]{2,1,0:T(8,128)} copy(s32[1,16,3]{1,0,2:T(1,128)} %param.14) | data formatting | bytes 384 | tf_op jit(solution)/shard_map/squeeze | solution.py:414
  3.2 5.3 %scatter.1 = (f32[3,32,32,128]{3,2,1,0:T(8,128)}, f32[3,32,32,128]{3,2,1,0:T(8,128)}) custom-call(s32[16,3]{1,0:T(8,128)} %bitcast.20, f32[3,16]{1,0:T(4,128)} %bitcast.21, s32[96,128]{1,0:T(8,128)} %bitcast.18, f32[96,128]{1,0:T(8,128)} %bitcast.19), custom_call_target="tpu_custom_call" | custom-call | tf_op jit(solution)/shard_map/scatter/pallas_call | solution.py:406
  8.5 70.4 %window.1 = (f32[32,32,128]{2,1,0:T(8,128)}, f32[32,32,128]{2,1,0:T(8,128)}, f32[32,32,128]{2,1,0:T(8,128)}) custom-call(f32[32,32,128]{2,1,0:T(8,128)} %bitcast.14, f32[32,32,128]{2,1,0:T(8,128)} %bitcast.15, f32[32,32,128]{2,1,0:T(8,128)} %bitcast.16, f32[32,32,128]{2,1,0:T(8,128)} %bitcast.17, f32[32,32,128]{2,1,0:T(8,128)} %courant.1, ...), custom_call_target="tpu_custom_call" | custom-call | tf_op jit(solution)/shard_map/window/pallas_call | solution.py:417
  79.0 2.2 %finish.1 = (f32[32,32,128]{2,1,0:T(8,128)}, f32[32,32,128]{2,1,0:T(8,128)}, f32[32,32,128]{2,1,0:T(8,128)}) custom-call(f32[32,32,128]{2,1,0:T(8,128)} %get-tuple-element.13.a, f32[32,32,128]{2,1,0:T(8,128)} %get-tuple-element.14.b, f32[32,32,128]{2,1,0:T(8,128)} %get-tuple-element.15.c), custom_call_target="tpu_custom_call" | custom-call | tf_op jit(solution)/shard_map/finish/pallas_call | solution.py:452

commit v4 on v3

--- a/solution.py
+++ b/solution.py
@@ -33,18 +33,18 @@
     depth_ids = lax.broadcasted_iota(jnp.int32, (1, LANES), 1)
 
     def one_source(i, carry):
-        x = scells[i, 0] - base_x
-        y = scells[i, 1] - base_y
+        x = scells[0, 0, i] - base_x
+        y = scells[1, 0, i] - base_y
 
         @pl.when((x >= 0) & (x < rows_x) & (y >= 0) & (y < rows_y))
         def _():
             for step in range(STEPS):
                 line = out_p[step, x, pl.ds(y, 1), :]
-                out_p[step, x, pl.ds(y, 1), :] = line + jnp.where(depth_ids == scells[i, 2], swave[step, i], 0.0)
+                out_p[step, x, pl.ds(y, 1), :] = line + jnp.where(depth_ids == scells[2, 0, i], swave[step, 0, i], 0.0)
 
         return carry
 
-    lax.fori_loop(0, scells.shape[0], one_source, 0)
+    lax.fori_loop(0, scells.shape[2], one_source, 0)
 
     x = (cells_ref[0:chunks, :] - base_x).astype(f32)
     y = (cells_ref[chunks : 2 * chunks, :] - base_y).astype(f32)
@@ -411,7 +411,7 @@
         scratch_shapes=[pltpu.VMEM((chunks, LANES), f32), pltpu.VMEM((16 * chunks, LANES), f32)],
         compiler_params=pltpu.CompilerParams(vmem_limit_bytes=WINDOW_LIMIT),
         name="scatter",
-    )(source_cells[0], source_wave[0], cells, values)
+    )(jnp.transpose(source_cells, (2, 0, 1)), jnp.transpose(source_wave, (1, 0, 2)), cells, values)
     sizes = (n_shot, n_gx, n_gy, rx, ry)
     dma = pltpu.SemaphoreType.DMA
     out_p, out_q, out_g = pl.pallas_call(

time: 81.4 us -> 78.6 us (0.966)
  local copies, waits for them, and re-layouts: 2.61 us -> 0 us
    squeeze x1 -> x0, local copies, waits for them, and re-layouts: 1.35 us -> none  [shards(): source_cells[0]]
    unnamed x1 -> x0, local copies, waits for them, and re-layouts: 1.26 us -> none
where the time goes in v4:
time: 78.6 us; the launch traced here: 78.4 us
  Pallas kernels  77.7 us (99%)
    pallas_call x1, Pallas kernels, shards(): pl.pallas_call(functools.partial(wave_kernel, sizes), out_shape=(block, b...  70.2 us
    pallas_call x1, Pallas kernels, shards(): pl.pallas_call(functools.partial(scatter_kernel, rx, ry, chunks), out_sha...  5.26 us
    pallas_call x1, Pallas kernels, shards(): pl.pallas_call(finish_kernel, out_shape=(block, block, block), in_specs=[...  2.23 us

profile of v4, /device:TPU:120, one launch (start us, length us, event | category | flops | bytes accessed | tf_op | source)
XLA Modules:
  0.0 78.4 jit_solution(16986171635056779441)
XLA Ops:
  0.6 5.3 %scatter.1 = (f32[3,32,32,128]{3,2,1,0:T(8,128)}, f32[3,32,32,128]{3,2,1,0:T(8,128)}) custom-call(s32[3,1,16]{2,1,0:T(1,128)} %bitcast.18, f32[3,1,16]{2,1,0:T(1,128)} %bitcast.19, s32[96,128]{1,0:T(8,128)} %bitcast.16, f32[96,128]{1,0:T(8,128)} %bitcast.17), custom_call_target="tpu_custom_call" | custom-call | tf_op jit(solution)/shard_map/scatter/pallas_call | solution.py:406
  5.9 70.2 %window.1 = (f32[32,32,128]{2,1,0:T(8,128)}, f32[32,32,128]{2,1,0:T(8,128)}, f32[32,32,128]{2,1,0:T(8,128)}) custom-call(f32[32,32,128]{2,1,0:T(8,128)} %bitcast.12, f32[32,32,128]{2,1,0:T(8,128)} %bitcast.13, f32[32,32,128]{2,1,0:T(8,128)} %bitcast.14, f32[32,32,128]{2,1,0:T(8,128)} %bitcast.15, f32[32,32,128]{2,1,0:T(8,128)} %courant.1, ...), custom_call_target="tpu_custom_call" | custom-call | tf_op jit(solution)/shard_map/window/pallas_call | solution.py:417
  76.1 2.2 %finish.1 = (f32[32,32,128]{2,1,0:T(8,128)}, f32[32,32,128]{2,1,0:T(8,128)}, f32[32,32,128]{2,1,0:T(8,128)}) custom-call(f32[32,32,128]{2,1,0:T(8,128)} %get-tuple-element.13.a, f32[32,32,128]{2,1,0:T(8,128)} %get-tuple-element.14.b, f32[32,32,128]{2,1,0:T(8,128)} %get-tuple-element.15.c), custom_call_target="tpu_custom_call" | custom-call | tf_op jit(solution)/shard_map/finish/pallas_call | solution.py:452

commit v5 on v4

--- a/solution.py
+++ b/solution.py
@@ -271,12 +271,14 @@
             final[f, x] = fresh
 
     def planes(step, f, low, high):
+        turn = 2 * UNROLL if (high - low) % (2 * UNROLL) == 0 else UNROLL
+
         def body(i, carry):
-            for k in range(UNROLL):
-                advance(step, f, low + i * UNROLL + k)
+            for k in range(turn):
+                advance(step, f, low + i * turn + k)
             return carry
 
-        lax.fori_loop(0, (high - low) // UNROLL, body, 0)
+        lax.fori_loop(0, (high - low) // turn, body, 0)
 
     for f in range(2):
         start_x(0, f)

time: 78.6 us -> 78.4 us (level)
  no operation moved by 1% of the time
where the time goes in v5:
time: 78.4 us; the launch traced here: 78.2 us
  Pallas kernels  77.5 us (99%)
    pallas_call x1, Pallas kernels, shards(): pl.pallas_call(functools.partial(wave_kernel, sizes), out_shape=(block, b...  70 us
    pallas_call x1, Pallas kernels, shards(): pl.pallas_call(functools.partial(scatter_kernel, rx, ry, chunks), out_sha...  5.26 us
    pallas_call x1, Pallas kernels, shards(): pl.pallas_call(finish_kernel, out_shape=(block, block, block), in_specs=[...  2.23 us

profile of v5, /device:TPU:120, one launch (start us, length us, event | category | flops | bytes accessed | tf_op | source)
XLA Modules:
  0.0 78.2 jit_solution(16264676487376663254)
XLA Ops:
  0.6 5.3 %scatter.1 = (f32[3,32,32,128]{3,2,1,0:T(8,128)}, f32[3,32,32,128]{3,2,1,0:T(8,128)}) custom-call(s32[3,1,16]{2,1,0:T(1,128)} %bitcast.18, f32[3,1,16]{2,1,0:T(1,128)} %bitcast.19, s32[96,128]{1,0:T(8,128)} %bitcast.16, f32[96,128]{1,0:T(8,128)} %bitcast.17), custom_call_target="tpu_custom_call" | custom-call | tf_op jit(solution)/shard_map/scatter/pallas_call | solution.py:408
  5.9 70.0 %window.1 = (f32[32,32,128]{2,1,0:T(8,128)}, f32[32,32,128]{2,1,0:T(8,128)}, f32[32,32,128]{2,1,0:T(8,128)}) custom-call(f32[32,32,128]{2,1,0:T(8,128)} %bitcast.12, f32[32,32,128]{2,1,0:T(8,128)} %bitcast.13, f32[32,32,128]{2,1,0:T(8,128)} %bitcast.14, f32[32,32,128]{2,1,0:T(8,128)} %bitcast.15, f32[32,32,128]{2,1,0:T(8,128)} %courant.1, ...), custom_call_target="tpu_custom_call" | custom-call | tf_op jit(solution)/shard_map/window/pallas_call | solution.py:419
  75.9 2.2 %finish.1 = (f32[32,32,128]{2,1,0:T(8,128)}, f32[32,32,128]{2,1,0:T(8,128)}, f32[32,32,128]{2,1,0:T(8,128)}) custom-call(f32[32,32,128]{2,1,0:T(8,128)} %get-tuple-element.13.a, f32[32,32,128]{2,1,0:T(8,128)} %get-tuple-element.14.b, f32[32,32,128]{2,1,0:T(8,128)} %get-tuple-element.15.c), custom_call_target="tpu_custom_call" | custom-call | tf_op jit(solution)/shard_map/finish/pallas_call | solution.py:454
